TPU v7x, 256 devices: a whole 4x4x8 slice. The times are simulated.
256 devices in a mesh: sec: 4 (over y_lo, core), tile: 64 (over x, y_hi, z).
Axes of the slice: x: 4, y: 4 (y_hi: 2, y_lo: 2; y = y_hi * 2 + y_lo), z: 8, core: 2. Of those that a mesh axis runs over, the one named last changes fastest.
Arguments:
- parent_old: float32 [1024, 24, 4096], P('tile', None, 'sec'), may hold values from -6 to 6
- nest_state: float32 [4, 1024, 24, 512], P('sec', 'tile'), may hold values from -6 to 6
- diffusion: float32 [24], replicated, may hold values from 0.04 to 0.1
- wind_speed: float32 [2, 24], replicated, may hold values from 0.05 to 0.25
- conversion: float32 [2, 8], replicated, may hold values from 0.05 to 0.4
- vert_mix: float32 [3], replicated, may hold values from 0.5 to 4
- nest_box: int32 [4, 4], replicated, may hold values from 0 to 3968, as said below
Outputs:
- parent_new: float32 [1024, 24, 4096], P('tile', None, 'sec')
- nest_new: float32 [4, 1024, 24, 512], P('sec', 'tile')
Inputs may be any that keep to these rules, and one draw needn't show every extreme that they name: `nest_box`: row n belongs to nest n, which lives on section n. Anchors are parent cells and keep the footprint of 256 by 128 parent cells inside the parent grid; live rows lie between 512 and 1024, live columns between 256 and 512; some nest is live everywhere.
All inputs are finite; a program needn't handle non-finite values.
Results may differ from a plain program's by a relative error of at most 0.00002.
Values sent between devices are 32-bit elements; how exact they have to be, the bound alone decides.
A program may use at most 64 MiB of HBM per device.

v0:
```python
import jax
import jax.numpy as jnp
from jax import lax
from jax.sharding import Mesh
from jax.sharding import PartitionSpec as P

NSTEP = 4
TILE = ("tile_0", "tile_1", "tile_2")


def with_halo(array, sides, width):
    edges = {}
    for axis, dim in sides:
        devices, length = (lax.axis_size(axis), array.shape[dim])
        up = [(i, (i + 1) % devices) for i in range(devices - 1)]
        last = lax.slice_in_dim(array, length - width, length, axis=dim)
        leading = lax.slice_in_dim(array, 0, width, axis=dim)
        edges[dim] = (
            lax.ppermute(last, axis, up),
            lax.ppermute(leading, axis, [(b, a) for a, b in up]),
        )
    done = []
    for _, dim in sides:
        low, high = edges[dim]
        around = [(width, width) if d in done else (0, 0) for d in range(array.ndim)]
        array = jnp.concatenate([jnp.pad(low, around), array, jnp.pad(high, around)], axis=dim)
        done.append(dim)
    return array


def split_up(array, dim, devices):
    before, after = (array.shape[:dim], array.shape[dim + 1 :])
    return jnp.moveaxis(array.reshape(*before, devices, -1, *after), dim, 0)


def sent_and_summed(array, axis, dim):
    devices = lax.axis_size(axis)
    parts = lax.all_to_all(split_up(array, dim, devices), axis, 0, 0, tiled=True)
    return jnp.sum(parts, axis=0)


def sum_in_order(parts, axes, sequence):
    shape = [lax.axis_size(a) for a in axes]
    parts = parts.reshape(*shape, *parts.shape[1:])
    parts = parts.transpose(*sequence, *range(len(axes), parts.ndim))
    parts = parts.reshape(-1, *parts.shape[len(axes) :])
    for k in sequence:
        parts = lax.psum_scatter(parts, axes[k], scatter_dimension=0, tiled=True)
    return parts[0]


def sum_by_axis(array, axes, sequence, dim):
    devices = lax.axis_size(axes)
    return sum_in_order(split_up(array, dim, devices), axes, sequence)


def extended_2(block, sides, width):
    for axis, dim in sides:
        count = lax.axis_size(axis)
        forward = [(i, i + 1) for i in range(count - 1)]
        backward = [(target, source) for source, target in forward]
        low = lax.ppermute(
            lax.slice_in_dim(block, block.shape[dim] - width, None, axis=dim), axis, forward
        )
        high = lax.ppermute(lax.slice_in_dim(block, 0, width, axis=dim), axis, backward)
        block = jnp.concatenate([low, block, high], axis=dim)
    return block


def horizontal(padded, diffusion, wind_speed):
    center = padded[1:-1, :, 1:-1]
    above_row = padded[:-2, :, 1:-1]
    below_row = padded[2:, :, 1:-1]
    left_col = padded[1:-1, :, :-2]
    right_col = padded[1:-1, :, 2:]
    spread = diffusion[:, None]
    drift_x = wind_speed[0][:, None]
    drift_y = wind_speed[1][:, None]
    return (
        center
        + spread * (above_row + below_row + left_col + right_col - 4.0 * center)
        - drift_x * (center - above_row)
        - drift_y * (center - left_col)
    )


def vertical(column_data, mixing):
    levels = column_data.shape[1]
    off_diag = -mixing
    ratios = []
    partials = []
    for level_idx in range(levels):
        neighbours = 1.0 if level_idx in (0, levels - 1) else 2.0
        pivot_val = 1.0 + neighbours * mixing
        rhs_now = column_data[:, level_idx]
        if level_idx > 0:
            pivot_val = pivot_val - off_diag * ratios[-1]
            rhs_now = rhs_now - off_diag * partials[-1]
        ratios.append(off_diag / pivot_val)
        partials.append(rhs_now / pivot_val)
    solved = [partials[-1]]
    for level_idx in range(levels - 2, -1, -1):
        solved.insert(0, partials[level_idx] - ratios[level_idx] * solved[0])
    return jnp.stack(solved, axis=1)


def physics(fields, conversion, vert_mix):
    row_count, chan_count, col_count = fields.shape
    levels = conversion.shape[1]
    grouped = fields.reshape(row_count, 3, levels, col_count)
    vapour = grouped[:, 0]
    cloud = grouped[:, 1]
    rain_water = grouped[:, 2]
    condense = conversion[0][:, None] * vapour
    vapour = vapour - condense
    cloud = cloud + condense
    fallout = conversion[1][:, None] * cloud
    cloud = cloud - fallout
    rain_water = rain_water + fallout
    solved = [
        vertical(vapour, vert_mix[0]),
        vertical(cloud, vert_mix[1]),
        vertical(rain_water, vert_mix[2]),
    ]
    return jnp.stack(solved, axis=1).reshape(row_count, chan_count, col_count)


def upsample(coarse, base, targets, foot_rows, foot_cols, nest_cols):
    low_row = jnp.floor_divide(targets, 4)
    weight_row = ((targets - 4 * low_row).astype(jnp.float32) / 4.0)[:, None, None]
    first_row = jnp.clip(low_row, 0, foot_rows - 1)
    second_row = jnp.clip(low_row + 1, 0, foot_rows - 1)
    lower_vals = jnp.take(coarse, first_row - base, axis=0)
    upper_vals = jnp.take(coarse, second_row - base, axis=0)
    row_mix = lower_vals + weight_row * (upper_vals - lower_vals)
    col_ids = jnp.arange(nest_cols, dtype=jnp.int32)
    first_col = jnp.floor_divide(col_ids, 4)
    second_col = jnp.minimum(first_col + 1, foot_cols - 1)
    weight_col = (col_ids - 4 * first_col).astype(jnp.float32) / 4.0
    left_vals = jnp.take(row_mix, first_col, axis=2)
    right_vals = jnp.take(row_mix, second_col, axis=2)
    return left_vals + weight_col * (right_vals - left_vals)


def nest_fields(targets, nest_cols, extent_x, extent_y):
    row_ids = targets[:, None]
    col_ids = jnp.arange(nest_cols, dtype=jnp.int32)[None, :]
    live_mask = ((row_ids >= 0) & (row_ids < extent_x) & (col_ids < extent_y)).astype(jnp.float32)
    distance = jnp.minimum(
        jnp.minimum(row_ids, col_ids), jnp.minimum(extent_x - 1 - row_ids, extent_y - 1 - col_ids)
    )
    distance = jnp.maximum(distance, 0).astype(jnp.float32)
    nudging = 0.1 + 0.4 * jnp.exp(-distance / 3.0)
    return (live_mask[:, None, :], nudging[:, None, :])


def nest_step(
    rows_padded, live_mask, nudging, forcing_now, diffusion, wind_speed, conversion, vert_mix
):
    padded = jnp.pad(rows_padded, ((0, 0), (0, 0), (1, 1)))
    moved = physics(horizontal(padded, diffusion, wind_speed), conversion, vert_mix)
    moved = moved + nudging * (forcing_now - moved)
    return moved * live_mask


def body(parent_old, nest_state, diffusion, wind_speed, conversion, vert_mix, nest_box):
    sec_pos = lax.axis_index("sec")
    tile_pos = lax.axis_index(TILE)
    tile_count = lax.axis_size(TILE)
    rows_tile, chan_count, cols_sec = parent_old.shape
    nest_rows = nest_state.shape[1]
    nest_cols = nest_state.shape[3]
    nest_count = nest_box.shape[0]
    own_rows = nest_rows // 4
    foot_rows = own_rows * tile_count
    foot_cols = nest_cols // 4
    my_box = nest_box[sec_pos]
    anchor_x = my_box[0]
    extent_x = my_box[2]
    extent_y = my_box[3]
    padded = with_halo(parent_old, (("sec", 2), (TILE, 0)), 1)
    parent_new = physics(horizontal(padded, diffusion, wind_speed), conversion, vert_mix)
    both_times = jnp.concatenate([parent_old, parent_new], axis=1)
    margin = 0
    send_chan = both_times.shape[1]
    strip_width = foot_cols + 2 * margin
    col_ids = (
        nest_box[:, 1][:, None]
        - margin
        + jnp.arange(strip_width, dtype=jnp.int32)[None, :]
        - sec_pos * cols_sec
    )
    col_valid = ((col_ids >= 0) & (col_ids < cols_sec)).astype(jnp.float32)
    picked = jnp.take(both_times, jnp.clip(col_ids, 0, cols_sec - 1).reshape(-1), axis=2)
    picked = picked.reshape(rows_tile, send_chan, nest_count, strip_width) * col_valid[None, None]
    routed = sent_and_summed(picked, "sec", 2)
    col_strip = routed.reshape(rows_tile, send_chan, strip_width)
    row_ids = (
        anchor_x
        + jnp.arange(own_rows * lax.axis_size(TILE), dtype=jnp.int32)
        - tile_pos * rows_tile
    )
    row_valid = ((row_ids >= 0) & (row_ids < rows_tile)).astype(jnp.float32)
    taken = jnp.take(col_strip, jnp.clip(row_ids, 0, rows_tile - 1), axis=0)
    routed_rows = sum_by_axis(taken * row_valid[:, None, None], TILE, (0, 2, 1), 0)
    reach = NSTEP // 4 + 1
    extended = extended_2(routed_rows, ((TILE, 0),), reach)
    targets = tile_pos * nest_rows - NSTEP + jnp.arange(nest_rows + 2 * NSTEP, dtype=jnp.int32)
    forcing = upsample(
        extended, tile_pos * own_rows - reach, targets, foot_rows, foot_cols, nest_cols
    )
    live_mask, nudging = nest_fields(targets, nest_cols, extent_x, extent_y)
    forcing_old = forcing[:, :chan_count]
    forcing_new = forcing[:, chan_count:]
    wide_state = extended_2(nest_state[0], ((TILE, 0),), NSTEP)
    wide_state = wide_state * live_mask
    for step_num in range(NSTEP):
        weight_now = (step_num + 1) / NSTEP
        forcing_now = forcing_old + weight_now * (forcing_new - forcing_old)
        rows_padded = jnp.pad(wide_state, ((1, 1), (0, 0), (0, 0)))
        wide_state = nest_step(
            rows_padded,
            live_mask,
            nudging,
            forcing_now,
            diffusion,
            wind_speed,
            conversion,
            vert_mix,
        )
    result = wide_state[NSTEP : NSTEP + nest_rows]
    return (parent_new, result[None])


def solution(mesh):
    torus = Mesh(
        mesh.devices.reshape(mesh.shape["sec"], 4, 2, 8), ("sec", "tile_0", "tile_1", "tile_2")
    )
    in_specs = (P(TILE, None, "sec"), P("sec", TILE, None, None), P(), P(), P(), P(), P())
    out_specs = (P(TILE, None, "sec"), P("sec", TILE, None, None))
    return jax.shard_map(body, mesh=torus, in_specs=in_specs, out_specs=out_specs, check_vma=False)
```

profile of v0, /device:TPU:1, one launch (start us, length us, event | category | flops | bytes accessed | tf_op | source)
XLA Modules:
  0.0 279.2 jit_solution(1722522420595157605)
XLA Ops:
  7.2 1.2 fusion.227
  8.4 4.6 %collective-permute-start.1 = (f32[16,24,1]{2,1,0:T(8,128)S(1)}, f32[16,24,1]{2,1,0:T(8,128)S(1)}, u32[]{:S(2)}, u32[]{:S(2)}) collective-permute-start(f32[16,24,1]{2,1,0:T(8,128)S(1)} %get-tuple-element.132), channel_id=1, source_target_pairs={{0,64},{64,128},{128,192},{1,65},{65,129},{129,193},{2,66},{66,130... | collective-permute-start | bytes 4616 | tf_op jit(solution)/shard_map/ppermute | solution.py:19
  13.0 1.9 collective-permute-start.2
  14.9 1.6 fusion.226
  16.5 4.2 %collective-permute-start = (f32[1,24,1024]{2,1,0:T(8,128)}, f32[1,24,1024]{2,1,0:T(8,128)}, u32[]{:S(2)}, u32[]{:S(2)}) collective-permute-start(f32[1,24,1024]{2,1,0:T(8,128)} %get-tuple-element.130), channel_id=1, source_target_pairs={{0,1},{1,2},{2,3},{3,4},{4,5},{5,6},{6,7},{7,8},{8,9},{9,10},{10,1... | collective-permute-start | bytes 294920 | tf_op jit(solution)/shard_map/ppermute | solution.py:19
  20.7 1.3 collective-permute-start.3
  30.4 2.2 concatenate.25
  32.7 2.7 fusion.8
  39.4 2.0 pad_maximum_fusion
  41.5 7.9 %copy.218 = f32[16,48,1024]{1,0,2:T(8,128)} copy(f32[16,48,1024]{2,1,0:T(8,128)} %pad_maximum_fusion) | data formatting | bytes 6291456 | tf_op jit(solution)/shard_map/concatenate | solution.py:183
  49.4 6.4 %gather_fusion = f32[512,16,48]{2,1,0:T(8,128)} fusion(f32[16,48,1024]{1,0,2:T(8,128)} %copy.218, s32[1024]{0:T(1024)S(1)} %copy-done.15), kind=kCustom, calls=%fused_computation.4 | custom fusion | bytes 3147776 | tf_op jit(solution)/shard_map/jit(_take)/gather | solution.py:194
  55.8 3.1 %copy.219 = f32[16,48,4,1,128]{4,1,3,0,2:T(8,128)S(1)} copy(f32[16,48,4,1,128]{1,0,4,2,3:T(8,128)} %bitcast.222) | data formatting | bytes 3145728 | tf_op jit(solution)/shard_map/jit(_take)/gather | solution.py:194
  58.9 1.3 multiply_bitcast_fusion.1
  60.2 3.7 %all-to-all-start = ((f32[4,16,48,1,128]{4,2,3,1,0:T(8,128)}), f32[4,16,48,1,128]{4,2,3,1,0:T(8,128)S(1)}, u32[]{:S(2)}, u32[]{:S(2)}) async-start(f32[4,16,48,1,128]{4,2,3,1,0:T(8,128)} %multiply_bitcast_fusion.1), calls=%async_computation | async-start | bytes 3145728 | tf_op jit(solution)/shard_map/all_to_all | solution.py:38
  66.6 16.2 %all-to-all-done = f32[4,16,48,1,128]{4,2,3,1,0:T(8,128)S(1)} async-done(((f32[4,16,48,1,128]{4,2,3,1,0:T(8,128)}), f32[4,16,48,1,128]{4,2,3,1,0:T(8,128)S(1)}, u32[]{:S(2)}, u32[]{:S(2)}) %all-to-all-start) | async-done | bytes 1572896 | tf_op jit(solution)/shard_map/all_to_all | solution.py:38
  82.8 3.7 %gather_fusion.1 = f32[256,48,128]{2,1,0:T(8,128)} fusion(f32[16,48,128]{2,1,0:T(8,128)S(1)} %reduce_sum.9, s32[1024]{0:T(1024)S(1)} %pad_clamp_fusion.4), kind=kCustom, calls=%fused_computation.5 | custom fusion | bytes 12583936 | tf_op jit(solution)/shard_map/jit(_take)/gather | solution.py:204
  86.6 3.2 %multiply_bitcast_fusion = f32[4,8,2,4,48,128]{5,4,3,1,2,0:T(8,128)S(1)} fusion(f32[4,2,8,4,48,128]{5,4,3,2,1,0:T(8,128)} %bitcast.221, f32[4,2,8,4]{3,2,1,0:T(8,128)S(1)} %get-tuple-element.179, pred[4,2,8,4]{3,2,1,0:T(8,128)(4,1)S(1)} %get-tuple-element.180), kind=kLoop, calls=%fused_computation.6 | loop fusion | flops 3145728 | bytes 12584192 | tf_op jit(solution)/shard_map/transpose | solution.py:45
  89.8 3.4 %copy.222 = f32[4,8,2,4,48,128]{5,4,3,2,1,0:T(8,128)} copy(f32[4,8,2,4,48,128]{5,4,3,1,2,0:T(8,128)S(1)} %multiply_bitcast_fusion) | data formatting | bytes 12582912 | tf_op jit(solution)/shard_map/transpose | solution.py:45
  94.3 4.3 %collective-permute-start.4 = (f32[4,24,512]{2,1,0:T(8,128)S(1)}, f32[4,24,512]{2,1,0:T(8,128)S(1)}, u32[]{:S(2)}, u32[]{:S(2)}) collective-permute-start(f32[4,24,512]{2,1,0:T(8,128)S(1)} %get-tuple-element.156), channel_id=1, source_target_pairs={{0,1},{1,2},{2,3},{3,4},{4,5},{5,6},{6,7},{7,8},{8,9},{9,10},{10,1... | collective-permute-start | bytes 589832 | tf_op jit(solution)/shard_map/ppermute | solution.py:62
  98.6 1.5 collective-permute-start.5
  110.6 53.7 %reduce-scatter.4.cloned.1.call-done = f32[16,4,48,128]{3,2,1,0:T(8,128)} async-done(((f32[64,4,48,128]{3,2,1,0:T(8,128)}), f32[16,4,48,128]{3,2,1,0:T(8,128)}) %reduce-scatter.4.cloned.1.call-update) | async-done | bytes 1572880 | tf_op jit(solution)/shard_map/reduce_scatter | solution.py:48
  164.9 38.9 %reduce-scatter.6.cloned.1.call-done = f32[2,4,48,128]{3,2,1,0:T(8,128)} async-done(((f32[16,4,48,128]{3,2,1,0:T(8,128)}), f32[2,4,48,128]{3,2,1,0:T(8,128)}) %reduce-scatter.6.cloned.1.call-update) | async-done | bytes 196624 | tf_op jit(solution)/shard_map/reduce_scatter | solution.py:48
  203.8 22.4 %reduce-scatter.8.cloned.1.call-done = f32[1,4,48,128]{3,2,1,0:T(8,128)} async-done(((f32[2,4,48,128]{3,2,1,0:T(8,128)}), f32[1,4,48,128]{3,2,1,0:T(8,128)}) %reduce-scatter.8.cloned.1.call-update) | async-done | bytes 98320 | tf_op jit(solution)/shard_map/reduce_scatter | solution.py:48
  227.1 3.2 %collective-permute-start.6 = (f32[2,48,128]{2,1,0:T(8,128)S(1)}, f32[2,48,128]{2,1,0:T(8,128)S(1)}, u32[]{:S(2)}, u32[]{:S(2)}) collective-permute-start(f32[2,48,128]{2,1,0:T(8,128)S(1)} %get-tuple-element.163), channel_id=1, source_target_pairs={{0,1},{1,2},{2,3},{3,4},{4,5},{5,6},{6,7},{7,8},{8,9},{9,10},{10,1... | collective-permute-start | bytes 147464 | tf_op jit(solution)/shard_map/ppermute | solution.py:62
  230.3 1.3 collective-permute-start.7
  231.7 3.4 %collective-permute-done.7 = f32[2,48,128]{2,1,0:T(8,128)S(1)} collective-permute-done((f32[2,48,128]{2,1,0:T(8,128)S(1)}, f32[2,48,128]{2,1,0:T(8,128)S(1)}, u32[]{:S(2)}, u32[]{:S(2)}) %collective-permute-start.7) | collective-permute-done | bytes 49184 | tf_op jit(solution)/shard_map/ppermute | solution.py:65
  237.5 3.8 %gather_fusion.4 = f32[512,24,48]{2,1,0:T(8,128)} fusion(f32[24,48,128]{1,0,2:T(8,128)S(1)} %copy.223, s32[1024]{0:T(1024)S(1)} %copy-done.14), kind=kCustom, calls=%fused_computation.1.clone | custom fusion | bytes 4720640 | tf_op jit(solution)/shard_map/jit(_take)/gather | solution.py:140
  241.3 5.8 %copy.224 = f32[512,24,48]{0,2,1:T(8,128)} copy(f32[512,24,48]{2,1,0:T(8,128)} %gather_fusion.4) | data formatting | bytes 4718592 | tf_op jit(solution)/shard_map/jit(_take)/gather | solution.py:140
  247.1 3.8 %gather_fusion.5 = f32[512,24,48]{2,1,0:T(8,128)} fusion(f32[24,48,128]{1,0,2:T(8,128)S(1)} %copy.223, s32[1024]{0:T(1024)S(1)} %copy-done.13), kind=kCustom, calls=%fused_computation.3.clone | custom fusion | bytes 4720640 | tf_op jit(solution)/shard_map/jit(_take)/gather | solution.py:141
  250.9 6.0 %copy.226 = f32[512,24,48]{0,2,1:T(8,128)} copy(f32[512,24,48]{2,1,0:T(8,128)} %gather_fusion.5) | data formatting | bytes 4718592 | tf_op jit(solution)/shard_map/jit(_take)/gather | solution.py:141
  256.9 2.3 fusion.1
  271.5 1.2 fusion.53
  (248 shorter events, 34.4 us)
Async XLA Ops:
  7.2 14.8 %copy-start.17 = (f32[3]{0:T(128)S(1)}, f32[3]{0:T(128)}, u32[]{:S(2)}) copy-start(f32[3]{0:T(128)} %param.16) | copy-start | bytes 40
  7.2 20.7 %copy-start.21 = (s32[4,4]{1,0:T(4,128)S(1)}, s32[4,4]{1,0:T(4,128)}, u32[]{:S(2)}) copy-start(s32[4,4]{1,0:T(4,128)} %param.17) | copy-start | bytes 196
  7.2 21.9 %copy-start.22 = (f32[2,24]{1,0:T(2,128)S(1)}, f32[2,24]{1,0:T(2,128)}, u32[]{:S(2)}) copy-start(f32[2,24]{1,0:T(2,128)} %param.14) | copy-start | bytes 580
  7.2 22.0 %copy-start.23 = (f32[2,8]{1,0:T(2,128)S(1)}, f32[2,8]{1,0:T(2,128)}, u32[]{:S(2)}) copy-start(f32[2,8]{1,0:T(2,128)} %param.15) | copy-start | bytes 196
  8.4 22.1 %collective-permute-start.1 = (f32[16,24,1]{2,1,0:T(8,128)S(1)}, f32[16,24,1]{2,1,0:T(8,128)S(1)}, u32[]{:S(2)}, u32[]{:S(2)}) collective-permute-start(f32[16,24,1]{2,1,0:T(8,128)S(1)} %get-tuple-element.132), channel_id=1, source_target_pairs={{0,64},{64,128},{128,192},{1,65},{65,129},{129,193},{2,66},{66,130... | collective-permute-start | bytes 4616 | tf_op jit(solution)/shard_map/ppermute | solution.py:19
  13.0 17.5 %collective-permute-start.2 = (f32[16,24,1]{2,1,0:T(8,128)S(1)}, f32[16,24,1]{2,1,0:T(8,128)}, u32[]{:S(2)}, u32[]{:S(2)}) collective-permute-start(f32[16,24,1]{2,1,0:T(8,128)S(1)} %get-tuple-element.133), channel_id=1, source_target_pairs={{64,0},{128,64},{192,128},{65,1},{129,65},{193,129},{66,2},{130,66... | collective-permute-start | bytes 4616 | tf_op jit(solution)/shard_map/ppermute | solution.py:20
  16.5 16.2 %collective-permute-start = (f32[1,24,1024]{2,1,0:T(8,128)}, f32[1,24,1024]{2,1,0:T(8,128)}, u32[]{:S(2)}, u32[]{:S(2)}) collective-permute-start(f32[1,24,1024]{2,1,0:T(8,128)} %get-tuple-element.130), channel_id=1, source_target_pairs={{0,1},{1,2},{2,3},{3,4},{4,5},{5,6},{6,7},{7,8},{8,9},{9,10},{10,1... | collective-permute-start | bytes 294920 | tf_op jit(solution)/shard_map/ppermute | solution.py:19
  20.7 12.0 %collective-permute-start.3 = (f32[1,24,1024]{2,1,0:T(8,128)}, f32[1,24,1024]{2,1,0:T(8,128)}, u32[]{:S(2)}, u32[]{:S(2)}) collective-permute-start(f32[1,24,1024]{2,1,0:T(8,128)} %get-tuple-element.131), channel_id=1, source_target_pairs={{1,0},{2,1},{3,2},{4,3},{5,4},{6,5},{7,6},{8,7},{9,8},{10,9},{11,1... | collective-permute-start | bytes 294920 | tf_op jit(solution)/shard_map/ppermute | solution.py:20
  30.4 2.3 copy-start
  38.3 1.1 copy-start.2
  41.5 7.9 %copy-start.15 = (s32[1024]{0:T(1024)S(1)}, s32[1024]{0:T(1024)}, u32[]{:S(2)}) copy-start(s32[1024]{0:T(1024)} %pad_clamp_fusion.5) | copy-start | bytes 12292
  55.8 3.1 %copy-start.16 = (f32[4,128]{1,0:T(4,128)S(1)}, f32[4,128]{1,0:T(4,128)}, u32[]{:S(2)}) copy-start(f32[4,128]{1,0:T(4,128)} %get-tuple-element.173) | copy-start | bytes 6148
  55.8 3.1 %copy-start.18 = (pred[4,128]{1,0:T(4,128)(4,1)S(1)}, pred[4,128]{1,0:T(4,128)(4,1)}, u32[]{:S(2)}) copy-start(pred[4,128]{1,0:T(4,128)(4,1)} %get-tuple-element.172) | copy-start | bytes 1540
  60.2 22.5 %all-to-all-start = ((f32[4,16,48,1,128]{4,2,3,1,0:T(8,128)}), f32[4,16,48,1,128]{4,2,3,1,0:T(8,128)S(1)}, u32[]{:S(2)}, u32[]{:S(2)}) async-start(f32[4,16,48,1,128]{4,2,3,1,0:T(8,128)} %multiply_bitcast_fusion.1), calls=%async_computation | async-start | bytes 3145728 | tf_op jit(solution)/shard_map/all_to_all | solution.py:38
  63.9 100.4 %reduce-scatter.4.cloned.1.call-start = ((), (), s32[]{:S(2)}) async-start(), calls=%async_computation.4 | async-start | bytes 7864320 | tf_op jit(solution)/shard_map/reduce_scatter | solution.py:48
  93.2 1.1 copy-start.3
  93.2 110.6 %reduce-scatter.6.cloned.1.call-start = ((), (), s32[]{:S(2)}) async-start(), calls=%async_computation.5 | async-start | bytes 1769472 | tf_op jit(solution)/shard_map/reduce_scatter | solution.py:48
  94.3 13.7 %collective-permute-start.4 = (f32[4,24,512]{2,1,0:T(8,128)S(1)}, f32[4,24,512]{2,1,0:T(8,128)S(1)}, u32[]{:S(2)}, u32[]{:S(2)}) collective-permute-start(f32[4,24,512]{2,1,0:T(8,128)S(1)} %get-tuple-element.156), channel_id=1, source_target_pairs={{0,1},{1,2},{2,3},{3,4},{4,5},{5,6},{6,7},{7,8},{8,9},{9,10},{10,1... | collective-permute-start | bytes 589832 | tf_op jit(solution)/shard_map/ppermute | solution.py:62
  98.6 9.4 %collective-permute-start.5 = (f32[4,24,512]{2,1,0:T(8,128)S(1)}, f32[4,24,512]{2,1,0:T(8,128)S(1)}, u32[]{:S(2)}, u32[]{:S(2)}) collective-permute-start(f32[4,24,512]{2,1,0:T(8,128)S(1)} %get-tuple-element.157), channel_id=1, source_target_pairs={{1,0},{2,1},{3,2},{4,3},{5,4},{6,5},{7,6},{8,7},{9,8},{10,9},{11,1... | collective-permute-start | bytes 589832 | tf_op jit(solution)/shard_map/ppermute | solution.py:65
  101.4 1.3 copy-start.6
  103.3 4.8 %copy-start.4 = (f32[24,512]{1,0:T(8,128)}, f32[24,512]{1,0:T(8,128)S(1)}, u32[]{:S(2)}) copy-start(f32[24,512]{1,0:T(8,128)S(1)} %and_convert_fusion) | copy-start | bytes 147460
  164.3 61.9 %reduce-scatter.8.cloned.1.call-start = ((), (), s32[]{:S(2)}) async-start(), calls=%async_computation.6 | async-start | bytes 294912 | tf_op jit(solution)/shard_map/reduce_scatter | solution.py:48
  227.1 4.6 %collective-permute-start.6 = (f32[2,48,128]{2,1,0:T(8,128)S(1)}, f32[2,48,128]{2,1,0:T(8,128)S(1)}, u32[]{:S(2)}, u32[]{:S(2)}) collective-permute-start(f32[2,48,128]{2,1,0:T(8,128)S(1)} %get-tuple-element.163), channel_id=1, source_target_pairs={{0,1},{1,2},{2,3},{3,4},{4,5},{5,6},{6,7},{7,8},{8,9},{9,10},{10,1... | collective-permute-start | bytes 147464 | tf_op jit(solution)/shard_map/ppermute | solution.py:62
  230.3 4.8 %collective-permute-start.7 = (f32[2,48,128]{2,1,0:T(8,128)S(1)}, f32[2,48,128]{2,1,0:T(8,128)S(1)}, u32[]{:S(2)}, u32[]{:S(2)}) collective-permute-start(f32[2,48,128]{2,1,0:T(8,128)S(1)} %get-tuple-element.164), channel_id=1, source_target_pairs={{1,0},{2,1},{3,2},{4,3},{5,4},{6,5},{7,6},{8,7},{9,8},{10,9},{11,1... | collective-permute-start | bytes 147464 | tf_op jit(solution)/shard_map/ppermute | solution.py:65
  231.6 3.5 %copy-start.8 = (f32[1,4,48,128]{3,2,1,0:T(8,128)S(1)}, f32[1,4,48,128]{3,2,1,0:T(8,128)}, u32[]{:S(2)}) copy-start(f32[1,4,48,128]{3,2,1,0:T(8,128)} %reduce-scatter.8.cloned.1.call-done) | copy-start | bytes 294916
  235.1 1.5 copy-start.19
  235.1 1.5 copy-start.20
  235.1 1.5 copy-start.24
  241.3 5.8 %copy-start.13 = (s32[1024]{0:T(1024)S(1)}, s32[1024]{0:T(1024)}, u32[]{:S(2)}) copy-start(s32[1024]{0:T(1024)} %get-tuple-element.187) | copy-start | bytes 12292
  250.9 6.0 %copy-start.1 = (f32[512,24,48]{0,2,1:T(8,128)S(1)}, f32[512,24,48]{0,2,1:T(8,128)}, u32[]{:S(2)}) copy-start(f32[512,24,48]{0,2,1:T(8,128)} %copy.224) | copy-start | bytes 7077892
  256.9 2.3 copy-start.5
  256.9 2.3 copy-start.7
  (5 other events, 3.5 us)
Sparse Core Ops, SparseCore 0:
  93.3 70.9 reduce-scatter.3
  166.9 36.8 reduce-scatter.5
  206.2 19.9 reduce-scatter.7
where the time goes:
time: 284 us; the launch traced here: 279 us
  waiting for transfers between devices  135 us (48%)
  local copies, waits for them, and re-layouts  61.4 us (22%)
  other arithmetic  34.5 us (12%)
  starting transfers between devices  25.9 us (9%)
  between operations  22.7 us (8%)
    reduce_scatter x3, waiting for transfers between devices, sum_in_order(): parts = lax.psum_scatter(parts, axes[k], scatter_dimension=0, tiled=True)  115 us
    all_to_all x1, waiting for transfers between devices, sent_and_summed(): lax.all_to_all(split_up(array, dim, devices), axis, 0, 0, tiled=True)  16.2 us
    gather x2, local copies, waits for them, and re-layouts, upsample(): right_vals = jnp.take(row_mix, second_col, axis=2)  9.79 us
    gather x2, local copies, waits for them, and re-layouts, upsample(): left_vals = jnp.take(row_mix, first_col, axis=2)  9.59 us
    gather x2, local copies, waits for them, and re-layouts, body(): jnp.take(both_times, jnp.clip(col_ids, 0, cols_sec - 1).reshape(-1), axis=2)  9.48 us
    ppermute x2, starting transfers between devices, with_halo(): lax.ppermute(last, axis, up)  8.75 us
    concatenate x1, local copies, waits for them, and re-layouts, body(): both_times = jnp.concatenate([parent_old, parent_new], axis=1)  7.91 us
    ppermute x2, starting transfers between devices, extended_2(): lax.ppermute(lax.slice_in_dim(block, block.shape[dim] - width, None, axis...  7.45 us
  transfers between devices with their start and end apart: 12, of which 5 were waited for; matrix products, arithmetic and copies ran while one was open for 6% of the time, Pallas kernels for 0%

commit v1 on v0

v1 whole, which is shorter than its diff:
```python
import itertools

import jax
import jax.numpy as jnp
from jax import lax
from jax.experimental import pallas as pl
from jax.experimental.pallas import tpu as pltpu
from jax.sharding import Mesh
from jax.sharding import PartitionSpec as P

NSTEP = 4
LEV = 8
SEC = ("yl", "co")
TILE = ("tx", "th", "tz")
LANES = 128
SLOT = 56
MESH = pl.DeviceIdType.MESH
F32 = jnp.float32


def vmem():
    return pl.BlockSpec(memory_space=pltpu.VMEM)


def smem():
    return pl.BlockSpec(memory_space=pltpu.SMEM)


def anywhere():
    return pl.BlockSpec(memory_space=pl.ANY)


def section():
    return lax.axis_index("yl") * 2 + lax.axis_index("co")


def tile_number():
    return lax.axis_index("tx") * 16 + lax.axis_index("th") * 8 + lax.axis_index("tz")


def lane_ids():
    return lax.broadcasted_iota(jnp.int32, (LEV, LANES), 1)


def level_ids():
    return lax.broadcasted_iota(jnp.int32, (LEV, LANES), 0)


def spread_out(column):
    return jnp.broadcast_to(column, (LEV, LANES))


def pack_kernel(box, parent, win, edge, pad, extra, sem):
    rows = parent.shape[0]
    cols = parent.shape[2]
    side = 3 * LANES
    sec = section()
    tile = tile_number()
    copy = pltpu.make_async_copy(parent, pad.at[:, :, pl.ds(side, cols)], sem)
    copy.start()
    pad[:, :, 0:side] = jnp.zeros((rows, 24, side), F32)
    pad[:, :, side + cols :] = jnp.zeros((rows, 24, side), F32)
    lane = lane_ids()
    level = level_ids()
    copy.wait()

    for which in range(2):
        at = side if which == 0 else side + cols - 1
        base, off = at // LANES * LANES, at % LANES
        for f in range(3):
            total = jnp.zeros((LEV, LANES), F32)
            for r in range(rows):
                piece = pad[r, pl.ds(8 * f, 8), pl.ds(base, LANES)]
                total = jnp.where(lane == r, spread_out(piece[:, off : off + 1]), total)
            edge[which, pl.ds(8 * f, 8), :] = total

    for order in range(4):
        nest = (order % 2) * 2 + order // 2
        ox = box[nest, 0]
        oy = box[nest, 1]
        start = jnp.clip(oy - cols * sec - 1, -side, cols + LANES - 1) + side
        block = start // LANES
        shift = start - block * LANES + 1
        back = (LANES - shift) % LANES

        def window(r, f):
            parts = []
            for q in range(3):
                piece = pad[r, pl.ds(8 * f, 8), pl.ds(pl.multiple_of((block + q) * LANES, LANES), LANES)]
                parts.append(pltpu.roll(piece, back, 1))
            inner = jnp.where(lane + shift < LANES, parts[0], parts[1])
            right = jnp.where(shift < LANES, parts[1][:, 0:1], parts[2][:, 0:1])
            return inner, parts[0][:, LANES - 1 : LANES], right

        def slot(k, carry):
            packed = jnp.zeros((LEV, LANES), F32)
            for par in range(2):
                r = 2 * k + par
                foot = rows * tile + r - ox
                keep = jnp.where((foot >= 0) & (foot < 256), 1.0, 0.0).astype(F32)
                for f in range(3):
                    inner, left, right = window(r, f)
                    win[order, k, pl.ds(24 * par + 8 * f, 8), :] = inner * keep
                    place = 12 * level + 4 * f + 2 * par
                    packed = jnp.where(lane == place, spread_out(left) * keep, packed)
                    packed = jnp.where(lane == place + 1, spread_out(right) * keep, packed)
            line = jnp.sum(packed, axis=0, keepdims=True)
            win[order, k, 48:56, :] = jnp.where(level == 6, jnp.broadcast_to(line, (LEV, LANES)), 0.0)
            return carry

        lax.fori_loop(0, rows // 2, slot, 0)

        for e, row in enumerate((ox - 1 - rows * tile, ox + 256 - rows * tile)):
            inside = (row >= 0) & (row < rows)
            keep = jnp.where(inside, 1.0, 0.0).astype(F32)
            r = jnp.clip(row, 0, rows - 1)
            for f in range(3):
                inner, _, _ = window(r, f)
                extra[pl.ds(24 * e + 8 * f, 8), :] = inner * keep
        for k in range(8):
            win[order, k, 48:54, :] = extra[6 * k : 6 * k + 6, :]


def move_kernel(box, win, edge, nest, parent, slots, low, high, rowhalo, colhalo, near, comb, gathered, summed, ready, sends,
                sem_s, sem_r, sem1_s, sem1_r, semz_s, semz_r, sem2_s, sem2_r):
    yl, co, tx, th, tz = (lax.axis_index(a) for a in ("yl", "co", "tx", "th", "tz"))
    mine = tx * 2 + th
    sec = yl * 2 + co
    tile = tx * 16 + th * 8 + tz
    here = dict(yl=yl, co=co, tx=tx, th=th, tz=tz)

    def tile_at(t):
        return dict(here, tx=t // 16, th=(t // 8) % 2, tz=t % 8)

    def sec_at(s):
        return dict(here, yl=s // 2, co=s % 2)

    core = dict(here, co=1 - co)
    following, before = tile_at((tile + 1) % 64), tile_at((tile + 63) % 64)
    east, west = sec_at((sec + 1) % 4), sec_at((sec + 3) % 4)
    cross = [
        (dict(here, tx=(tx + dx) % 4, th=(th + dh) % 2, yl=(yl + dl) % 2), dx, dh, dl)
        for dx, dh, dl in itertools.product((2, 1, 3, 0), (1, 0), (1, 0))
        if (dx, dh, dl) != (0, 0, 0)
    ]
    ring = [dict(here, tz=(tz + dz) % 8) for dz in (4, 3, 5, 2, 6, 1, 7)]
    greet = [core, following, before, east, west] + [c[0] for c in cross] + ring
    barrier = pltpu.get_barrier_semaphore()
    for device in greet:
        pl.semaphore_signal(barrier, inc=1, device_id=device, device_id_type=MESH)
    pl.semaphore_wait(barrier, len(greet))

    def send(src, dst, s, r, device):
        copy = pltpu.make_async_remote_copy(src_ref=src, dst_ref=dst, send_sem=s, recv_sem=r, device_id=device, device_id_type=MESH)
        copy.start()
        return copy

    first = send(win.at[pl.ds((1 - co) * 2, 2)], near, sem_s.at[0], sem_r.at[0], core)
    rows = nest.shape[1]
    last = parent.shape[0] - 1
    halos = [
        send(edge.at[1], colhalo.at[0], sem_s.at[1], sem_r.at[1], east),
        send(edge.at[0], colhalo.at[1], sem_s.at[2], sem_r.at[2], west),
        send(nest.at[0, pl.ds(rows - NSTEP, NSTEP)], low, sem_s.at[3], sem_r.at[3], following),
        send(nest.at[0, pl.ds(0, NSTEP)], high, sem_s.at[4], sem_r.at[4], before),
        send(parent.at[last], rowhalo.at[0], sem_s.at[5], sem_r.at[5], following),
        send(parent.at[0], rowhalo.at[1], sem_s.at[6], sem_r.at[6], before),
    ]
    first.wait()

    def combine(k, carry):
        for l in range(2):
            comb[l, k] = win[co * 2 + l, k] + near[l, k]
        return carry

    lax.fori_loop(0, 8, combine, 0)

    copies = []
    for j, (device, dx, dh, dl) in enumerate(cross):
        to = device["tx"] * 2 + device["th"]
        copies.append(send(comb.at[device["yl"], to], gathered.at[tx, yl, th], sem1_s.at[j], sem1_r.at[j], device))
    gathered[tx, yl, th] = comb[yl, mine]
    for copy in copies:
        copy.wait()
    for h in range(2):
        total = gathered[0, 0, h]
        for x, l in itertools.product(range(4), range(2)):
            if (x, l) != (0, 0):
                total = total + gathered[x, l, h]
        summed[tz, h] = total

    copies = [send(summed.at[tz], summed.at[tz], semz_s.at[j], semz_r.at[j], device) for j, device in enumerate(ring)]
    for copy in copies:
        copy.wait()

    lines = summed[0, 0, 48:56, :]
    for z, h in itertools.product(range(8), range(2)):
        if (z, h) != (0, 0):
            lines = lines + summed[z, h, 48:56, :]
    lines = jnp.where(level_ids() < 6, lines, 0.0)
    ox = box[sec, 0]

    def pick(device, where, slot):
        t = device["tx"] * 16 + device["th"] * 8 + tz
        q = ((ox + 4 * t + 254) % 256) // 2
        q = (q + (mine - q + 128) % 8) % 128
        z, h = (q // 8) % 8, q // 64
        where[slot, 0:48, :] = summed[z, h, 0:48, :]
        tail = summed[z, h, 48:56, :]
        where[slot, 48:56, :] = jnp.where(level_ids() < 6, lines, tail)

    copies = []
    j = 0
    for device, dx, dh, dl in cross:
        if dl == 0:
            pick(device, sends, j)
            copies.append(send(sends.at[j], ready.at[mine], sem2_s.at[j], sem2_r.at[j], device))
            j += 1
    pick(here, ready, mine)
    for copy in copies:
        copy.wait()
    for copy in halos:
        copy.wait()
    slots[...] = ready[...]


def fill_coefs(coef, diffusion, wind, conversion, mix):
    level = level_ids()

    def column(read):
        out = jnp.zeros((LEV, LANES), F32)
        for l in range(LEV):
            out = jnp.where(level == l, read(l), out)
        return out

    for f in range(3):
        d = column(lambda l: diffusion[8 * f + l])
        wx = column(lambda l: wind[0, 8 * f + l])
        wy = column(lambda l: wind[1, 8 * f + l])
        coef[f, 0] = 1.0 - 4.0 * d - wx - wy
        coef[f, 1] = d + wx
        coef[f, 2] = d
        coef[f, 3] = d + wy
        m = mix[f] * jnp.ones((LEV, LANES), F32)
        lower = jnp.where(level > 0, -m, 0.0)
        upper = jnp.where(level < LEV - 1, -m, 0.0)
        diag = 1.0 + m * jnp.where((level == 0) | (level == LEV - 1), 1.0, 2.0)
        item = 7
        for s in (1, 2, 4):
            alpha = -lower / pltpu.roll(diag, s, 0)
            gamma = -upper / pltpu.roll(diag, LEV - s, 0)
            new_diag = diag + alpha * pltpu.roll(upper, s, 0) + gamma * pltpu.roll(lower, LEV - s, 0)
            lower, upper = alpha * pltpu.roll(lower, s, 0), gamma * pltpu.roll(upper, LEV - s, 0)
            diag = new_diag
            if s < 4:
                coef[f, item] = alpha
                coef[f, item + 1] = gamma
                item += 2
            else:
                coef[f, item] = 1.0 / diag
                coef[f, item + 1] = (alpha + gamma) / diag
    c0 = column(lambda l: conversion[0, l])
    c1 = column(lambda l: conversion[1, l])
    coef[0, 4] = c0
    coef[0, 5] = 1.0 - c0
    coef[1, 4] = c1
    coef[1, 5] = 1.0 - c1


def solve(coef, f, r):
    r = r + coef[f, 7] * pltpu.roll(r, 1, 0) + coef[f, 8] * pltpu.roll(r, 7, 0)
    r = r + coef[f, 9] * pltpu.roll(r, 2, 0) + coef[f, 10] * pltpu.roll(r, 6, 0)
    return coef[f, 11] * r + coef[f, 12] * pltpu.roll(r, 4, 0)


def physics(coef, vapour, cloud, rain):
    wet = cloud + coef[0, 4] * vapour
    fields = (coef[0, 5] * vapour, coef[1, 5] * wet, rain + coef[1, 4] * wet)
    return [solve(coef, f, fields[f]) for f in range(3)]


def advance(coef, count, north, center, south, first, last):
    lane = lane_ids()
    moved = [[None] * count for _ in range(3)]
    for f in range(3):
        tiles = [center(f, q) for q in range(count)]
        right = [pltpu.roll(t, 1, 1) for t in tiles]
        left = [pltpu.roll(t, LANES - 1, 1) for t in tiles]
        for q in range(count):
            west = jnp.where(lane == 0, first(f) if q == 0 else right[q - 1], right[q])
            east = jnp.where(lane == LANES - 1, last(f) if q == count - 1 else left[q + 1], left[q])
            moved[f][q] = (coef[f, 0] * tiles[q] + coef[f, 1] * north(f, q) + coef[f, 2] * (south(f, q) + east)
                           + coef[f, 3] * west)
    for q in range(count):
        yield q, physics(coef, moved[0][q], moved[1][q], moved[2][q])


def nest_kernel(box, diffusion, wind, conversion, mix, slots, nest, low, high, out, coef, extra, old, new, flat, wide, state_a, state_b,
                keep, pull):
    sec = section()
    t = tile_number()
    rows = nest.shape[1]
    lane = lane_ids()
    level = level_ids()
    ox, ex, ey = box[sec, 0], box[sec, 2], box[sec, 3]
    fill_coefs(coef, diffusion, wind, conversion, mix)

    for k in range(8):
        extra[6 * k : 6 * k + 6, :] = slots[k, 48:54, :]

    def place(j):
        residue = (ox + 4 * t + 254 + j) % 256
        return (residue // 2) % 8, residue % 2

    for j in range(9):
        k, par = place(j)
        for f in range(3):
            old[j, pl.ds(8 * f, 8), :] = slots[k, pl.ds(pl.multiple_of(24 * par + 8 * f, 8), 8), :]

    @pl.when(t == 0)
    def _():
        old[1] = extra[0:24, :]

    @pl.when(t == 63)
    def _():
        old[6] = extra[24:48, :]

    for j in range(1, 8):
        k, par = place(j)
        line = jnp.broadcast_to(slots[k, 54:55, :], (LEV, LANES))

        def outer(f, which):
            at = 12 * level + 4 * f + 2 * par + which
            return spread_out(jnp.sum(jnp.where(lane == at, line, 0.0), axis=1, keepdims=True))

        read = lambda i: lambda f, q: old[i, pl.ds(8 * f, 8), :]
        for q, done in advance(coef, 1, read(j - 1), read(j), read(j + 1), lambda f: outer(f, 0), lambda f: outer(f, 1)):
            for f in range(3):
                new[j - 1, pl.ds(8 * f, 8), :] = done[f]

    @pl.when(t == 63)
    def _():
        old[6] = old[5]
        new[5] = new[4]

    for j in range(7):
        flat[pl.ds(24 * j, 24), :] = old[j + 1]
        flat[pl.ds(168 + 24 * j, 24), :] = new[j]

    cells = lax.broadcasted_iota(jnp.int32, (LANES, 512), 0)
    targets = lax.broadcasted_iota(jnp.int32, (LANES, 512), 1)
    weight = (targets % 4).astype(F32) * 0.25
    low_cell = targets // 4
    high_cell = jnp.minimum(low_cell + 1, LANES - 1)
    mixer = (jnp.where(cells == low_cell, 1.0 - weight, 0.0) + jnp.where(cells == high_cell, weight, 0.0)).astype(jnp.bfloat16)
    part = flat[...]
    total = None
    for _ in range(3):
        rounded = part.astype(jnp.bfloat16)
        product = jnp.dot(rounded, mixer, preferred_element_type=F32)
        total = product if total is None else total + product
        part = part - rounded.astype(F32)
    wide[...] = total

    wide_rows = rows + 2 * NSTEP
    row_id = rows * t - NSTEP + lax.broadcasted_iota(jnp.int32, (wide_rows, 512), 0)
    col_id = lax.broadcasted_iota(jnp.int32, (wide_rows, 512), 1)
    live = jnp.where((row_id >= 0) & (row_id < ex) & (col_id < ey), 1.0, 0.0).astype(F32)
    distance = jnp.minimum(jnp.minimum(row_id, col_id), jnp.minimum(ex - 1 - row_id, ey - 1 - col_id))
    nudging = 0.1 + 0.4 * jnp.exp(jnp.maximum(distance, 0).astype(F32) * (-1.0 / 3.0))
    kept, pulled = live * (1.0 - nudging), live * nudging
    for i in range(wide_rows):
        keep[i] = jnp.broadcast_to(kept[i : i + 1, :], (LEV, 512))
        pull[i] = jnp.broadcast_to(pulled[i : i + 1, :], (LEV, 512))

    def begin(src, i, at):
        alive = jnp.where(
            (rows * t - NSTEP + at >= 0) & (rows * t - NSTEP + at < ex) & (lax.broadcasted_iota(jnp.int32, (24, 512), 1) < ey), 1.0, 0.0
        ).astype(F32)
        state_a[at] = src[i] * alive

    for i in range(NSTEP):
        begin(low, i, i)
        begin(high, i, rows + NSTEP + i)

    def middle(i, carry):
        begin(nest.at[0], i, NSTEP + i)
        return carry

    lax.fori_loop(0, rows, middle, 0)

    zero = jnp.zeros((LEV, LANES), F32)
    states = (state_a, state_b)
    for step in range(1, NSTEP + 1):
        src, dst = states[(step - 1) % 2], states[step % 2]
        share = step / NSTEP

        def one_row(i, carry):
            u = i // 4
            p = (i % 4).astype(F32) * 0.25
            read = lambda k: lambda f, q: src[k, pl.ds(8 * f, 8), pl.ds(LANES * q, LANES)]
            for q, done in advance(coef, 4, read(i - 1), read(i), read(i + 1), lambda f: zero, lambda f: zero):
                columns = pl.ds(LANES * q, LANES)
                k_row, p_row = keep[i, :, columns], pull[i, :, columns]
                for f in range(3):
                    def force(v):
                        first = wide[pl.ds(pl.multiple_of(24 * v + 8 * f, 8), 8), columns]
                        if step == NSTEP:
                            return wide[pl.ds(pl.multiple_of(168 + 24 * v + 8 * f, 8), 8), columns]
                        second = wide[pl.ds(pl.multiple_of(168 + 24 * v + 8 * f, 8), 8), columns]
                        return first + share * (second - first)

                    before, after = force(u), force(u + 1)
                    result = k_row * done[f] + p_row * (before + p * (after - before))
                    if step == NSTEP:
                        out[0, i - NSTEP, pl.ds(8 * f, 8), columns] = result
                    else:
                        dst[i, pl.ds(8 * f, 8), columns] = result
            return carry

        lax.fori_loop(step, wide_rows - step, one_row, 0)


def parent_kernel(diffusion, wind, conversion, mix, parent, rowhalo, colhalo, out, coef):
    sec = section()
    t = tile_number()
    rows = parent.shape[0]
    count = parent.shape[2] // LANES
    lane = lane_ids()
    fill_coefs(coef, diffusion, wind, conversion, mix)
    have_up = jnp.where(t > 0, 1.0, 0.0).astype(F32)
    have_down = jnp.where(t < 63, 1.0, 0.0).astype(F32)
    have_left = jnp.where(sec > 0, 1.0, 0.0).astype(F32)
    have_right = jnp.where(sec < 3, 1.0, 0.0).astype(F32)

    def inner(i):
        return lambda f, q: parent[i, pl.ds(8 * f, 8), pl.ds(LANES * q, LANES)]

    def outer(side, scale):
        return lambda f, q: rowhalo[side, pl.ds(8 * f, 8), pl.ds(LANES * q, LANES)] * scale

    def one_row(i, north, south):
        def edge(side, scale):
            return lambda f: spread_out(
                jnp.sum(jnp.where(lane == i, colhalo[side, pl.ds(8 * f, 8), :], 0.0), axis=1, keepdims=True) * scale)

        for q, done in advance(coef, count, north, inner(i), south, edge(0, have_left), edge(1, have_right)):
            for f in range(3):
                out[i, pl.ds(8 * f, 8), pl.ds(LANES * q, LANES)] = done[f]

    one_row(0, outer(0, have_up), inner(1))

    def middle(i, carry):
        one_row(i, inner(i - 1), inner(i + 1))
        return carry

    lax.fori_loop(1, rows - 1, middle, 0)
    one_row(rows - 1, inner(rows - 2), outer(1, have_down))


def body(parent_old, nest_state, diffusion, wind_speed, conversion, vert_mix, nest_box):
    rows, chan, cols = parent_old.shape
    shape = jax.ShapeDtypeStruct
    win, edge = pl.pallas_call(
        pack_kernel,
        out_shape=(shape((4, 8, SLOT, LANES), F32), shape((2, chan, LANES), F32)),
        in_specs=[smem(), anywhere()],
        out_specs=(vmem(), vmem()),
        scratch_shapes=[pltpu.VMEM((rows, chan, cols + 6 * LANES), F32), pltpu.VMEM((48, LANES), F32), pltpu.SemaphoreType.DMA(())],
        name="pack",
    )(nest_box, parent_old)
    dma = pltpu.SemaphoreType.DMA
    slots, low, high, rowhalo, colhalo = pl.pallas_call(
        move_kernel,
        out_shape=(
            shape((8, SLOT, LANES), F32),
            shape((NSTEP, chan, nest_state.shape[3]), F32),
            shape((NSTEP, chan, nest_state.shape[3]), F32),
            shape((2, chan, cols), F32),
            shape((2, chan, LANES), F32),
        ),
        in_specs=[smem(), vmem(), vmem(), anywhere(), anywhere()],
        out_specs=(vmem(), anywhere(), anywhere(), anywhere(), anywhere()),
        scratch_shapes=[
            pltpu.VMEM((2, 8, SLOT, LANES), F32),
            pltpu.VMEM((2, 8, SLOT, LANES), F32),
            pltpu.VMEM((4, 2, 2, SLOT, LANES), F32),
            pltpu.VMEM((8, 2, SLOT, LANES), F32),
            pltpu.VMEM((8, SLOT, LANES), F32),
            pltpu.VMEM((7, SLOT, LANES), F32),
            dma((7,)), dma((7,)), dma((15,)), dma((15,)), dma((7,)), dma((7,)), dma((7,)), dma((7,)),
        ],
        compiler_params=pltpu.CompilerParams(collective_id=0, has_side_effects=True),
        name="move",
    )(nest_box, win, edge, nest_state, parent_old)
    nest_new = pl.pallas_call(
        nest_kernel,
        out_shape=shape(nest_state.shape, F32),
        in_specs=[smem()] * 5 + [vmem()] * 4,
        out_specs=vmem(),
        scratch_shapes=[
            pltpu.VMEM((3, 13, LEV, LANES), F32),
            pltpu.VMEM((48, LANES), F32),
            pltpu.VMEM((9, chan, LANES), F32),
            pltpu.VMEM((7, chan, LANES), F32),
            pltpu.VMEM((14 * chan, LANES), F32),
            pltpu.VMEM((14 * chan, 512), F32),
            pltpu.VMEM((24, chan, 512), F32),
            pltpu.VMEM((24, chan, 512), F32),
            pltpu.VMEM((24, LEV, 512), F32),
            pltpu.VMEM((24, LEV, 512), F32),
        ],
        name="nest",
    )(nest_box, diffusion, wind_speed, conversion, vert_mix, slots, nest_state, low, high)
    parent_new = pl.pallas_call(
        parent_kernel,
        out_shape=shape(parent_old.shape, F32),
        in_specs=[smem()] * 4 + [vmem()] * 3,
        out_specs=vmem(),
        scratch_shapes=[pltpu.VMEM((3, 13, LEV, LANES), F32)],
        name="parent",
    )(diffusion, wind_speed, conversion, vert_mix, parent_old, rowhalo, colhalo)
    return parent_new, nest_new


def solution(mesh):
    grid = Mesh(mesh.devices.reshape(2, 2, 4, 2, 8), SEC + TILE)
    in_specs = (P(TILE, None, SEC), P(SEC, TILE, None, None), P(), P(), P(), P(), P())
    out_specs = (P(TILE, None, SEC), P(SEC, TILE, None, None))
    return jax.shard_map(body, mesh=grid, in_specs=in_specs, out_specs=out_specs, check_vma=False)
```

time: 284 us -> 70.9 us (0.25); the launches traced: 279 us -> 69.9 us
  waiting for transfers between devices: 135 us -> 0 us
  Pallas kernels: 0 us -> 69.3 us
  local copies, waits for them, and re-layouts: 61.4 us -> 0 us
  other arithmetic: 34.5 us -> 0 us
  starting transfers between devices: 25.9 us -> 0 us
  between operations: 22.7 us -> 0.65 us
    reduce_scatter x3 -> x0, waiting for transfers between devices: 115 us -> none  [sum_in_order(): parts = lax.psum_scatter(parts, axes[k], scatter_dimension=0, tiled=True)]
    pallas_call x0 -> x4, Pallas kernels: none -> 69.3 us  [the longest x1 41.3 us: body(): pl.pallas_call(move_kernel, out_shape=(shape((8, SLOT, LANES), F32), shap...]
    gather x9 -> x0, local copies, waits for them, and re-layouts: 34 us -> none  [the longest x2 9.79 us: upsample(): right_vals = jnp.take(row_mix, second_col, axis=2)]
    ppermute x8 -> x0, starting transfers between devices: 22.2 us -> none  [the longest x2 8.75 us: with_halo(): lax.ppermute(last, axis, up)]
    all_to_all x1 -> x0, waiting for transfers between devices: 16.2 us -> none  [sent_and_summed(): lax.all_to_all(split_up(array, dim, devices), axis, 0, 0, tiled=True)]
    concatenate x2 -> x0, local copies, waits for them, and re-layouts: 10.1 us -> none  [the longest x1 7.91 us: body(): both_times = jnp.concatenate([parent_old, parent_new], axis=1)]
    slice x14 -> x0, local copies, waits for them, and re-layouts: 6.81 us -> none  [the longest x2 2.78 us: with_halo(): last = lax.slice_in_dim(array, length - width, length, axis=dim)]
    reshape x5 -> x0, other arithmetic: 6.38 us -> none  [physics(): grouped = fields.reshape(row_count, 3, levels, col_count)]
  transfers between devices with their start and end apart: 12 -> 0, of which waited for: 5 -> 0; matrix products, arithmetic and copies ran while one was open for 6% -> 0% of each run, Pallas kernels for 0% -> 0%
where the time goes in v1:
time: 70.9 us; the launch traced here: 69.9 us
  Pallas kernels  69.3 us (98%)
    pallas_call x1, Pallas kernels, body(): pl.pallas_call(move_kernel, out_shape=(shape((8, SLOT, LANES), F32), shap...  41.3 us
    pallas_call x1, Pallas kernels, body(): pl.pallas_call(nest_kernel, out_shape=shape(nest_state.shape, F32), in_sp...  13.3 us
    pallas_call x1, Pallas kernels, body(): pl.pallas_call(pack_kernel, out_shape=(shape((4, 8, SLOT, LANES), F32), s...  8.99 us
    pallas_call x1, Pallas kernels, body(): pl.pallas_call(parent_kernel, out_shape=shape(parent_old.shape, F32), in_...  5.66 us

profile of v1, /device:TPU:1, one launch (start us, length us, event | category | flops | bytes accessed | tf_op | source)
XLA Modules:
  0.0 69.9 jit_solution(17572243829199721836)
XLA Ops:
  0.6 9.0 %pack.1 = (f32[4,8,56,128]{3,2,1,0:T(8,128)}, f32[2,24,128]{2,1,0:T(8,128)}) custom-call(s32[4,4]{1,0:T(4,128)} %box.5, f32[16,24,1024]{2,1,0:T(8,128)} %parent.7), custom_call_target="tpu_custom_call" | custom-call | tf_op jit(solution)/shard_map/pack/pallas_call | solution.py:464
  9.6 41.3 %move.1 = (f32[8,56,128]{2,1,0:T(8,128)}, f32[4,24,512]{2,1,0:T(8,128)}, f32[4,24,512]{2,1,0:T(8,128)}, f32[2,24,1024]{2,1,0:T(8,128)}, f32[2,24,128]{2,1,0:T(8,128)}) custom-call(s32[4,4]{1,0:T(4,128)} %box.5, f32[4,8,56,128]{3,2,1,0:T(8,128)} %get-tuple-element.9.win, f32[2,24,128]{2,1,0:T(8,128)} %get-tuple-element.10.edge, f32[1,16,24,512]{3,2,1,0:T(8,128)} %nest.5, ...), custom_call_target="tpu_custom_call" | custom-call | tf_op jit(solution)/shard_map/move/pallas_call | solution.py:473
  50.9 13.3 %nest.4 = f32[1,16,24,512]{3,2,1,0:T(8,128)} custom-call(s32[4,4]{1,0:T(4,128)} %box.5, f32[24]{0:T(128)} %diffusion.3, f32[2,24]{1,0:T(2,128)} %wind.3, f32[2,8]{1,0:T(2,128)} %conversion.3, f32[3]{0:T(128)} %mix.3, f32[8,56,128]{2,1,0:T(8,128)} %get-tuple-element.13.slots, f32[1,16,24,512]{3,2,1,0:T(8,128)} %nest.5, f32[4,24,512]{2,1,0:T(8,128)} %get-tuple-element.14.low, ...), custom_call_target="tpu_custom_call" | custom-call | tf_op jit(solution)/shard_map/nest/pallas_call | solution.py:496
  64.3 5.7 %parent.6 = f32[16,24,1024]{2,1,0:T(8,128)} custom-call(f32[24]{0:T(128)} %diffusion.3, f32[2,24]{1,0:T(2,128)} %wind.3, f32[2,8]{1,0:T(2,128)} %conversion.3, f32[3]{0:T(128)} %mix.3, f32[16,24,1024]{2,1,0:T(8,128)} %parent.7, f32[2,24,1024]{2,1,0:T(8,128)} %get-tuple-element.11.rowhalo, f32[2,24,128]{2,1,0:T(8,128)} %get-tuple-element.12.colhalo), custom_call_target="tpu_custom_call" | custom-call | tf_op jit(solution)/shard_map/parent/pallas_call | solution.py:515

commit v2 on v1

--- a/solution.py
+++ b/solution.py
@@ -50,22 +50,10 @@
     return jnp.broadcast_to(column, (LEV, LANES))
 
 
-def pack_kernel(box, parent, win, edge, pad, extra, sem):
-    rows = parent.shape[0]
-    cols = parent.shape[2]
-    side = 3 * LANES
-    sec = section()
-    tile = tile_number()
-    copy = pltpu.make_async_copy(parent, pad.at[:, :, pl.ds(side, cols)], sem)
-    copy.start()
-    pad[:, :, 0:side] = jnp.zeros((rows, 24, side), F32)
-    pad[:, :, side + cols :] = jnp.zeros((rows, 24, side), F32)
+def pack_edges(pad, edge, rows, cols):
     lane = lane_ids()
-    level = level_ids()
-    copy.wait()
-
     for which in range(2):
-        at = side if which == 0 else side + cols - 1
+        at = 0 if which == 0 else cols - 1
         base, off = at // LANES * LANES, at % LANES
         for f in range(3):
             total = jnp.zeros((LEV, LANES), F32)
@@ -74,60 +62,68 @@
                 total = jnp.where(lane == r, spread_out(piece[:, off : off + 1]), total)
             edge[which, pl.ds(8 * f, 8), :] = total
 
-    for order in range(4):
-        nest = (order % 2) * 2 + order // 2
-        ox = box[nest, 0]
-        oy = box[nest, 1]
-        start = jnp.clip(oy - cols * sec - 1, -side, cols + LANES - 1) + side
-        block = start // LANES
-        shift = start - block * LANES + 1
-        back = (LANES - shift) % LANES
-
-        def window(r, f):
-            parts = []
-            for q in range(3):
-                piece = pad[r, pl.ds(8 * f, 8), pl.ds(pl.multiple_of((block + q) * LANES, LANES), LANES)]
-                parts.append(pltpu.roll(piece, back, 1))
-            inner = jnp.where(lane + shift < LANES, parts[0], parts[1])
-            right = jnp.where(shift < LANES, parts[1][:, 0:1], parts[2][:, 0:1])
-            return inner, parts[0][:, LANES - 1 : LANES], right
-
-        def slot(k, carry):
-            packed = jnp.zeros((LEV, LANES), F32)
-            for par in range(2):
-                r = 2 * k + par
-                foot = rows * tile + r - ox
-                keep = jnp.where((foot >= 0) & (foot < 256), 1.0, 0.0).astype(F32)
-                for f in range(3):
-                    inner, left, right = window(r, f)
-                    win[order, k, pl.ds(24 * par + 8 * f, 8), :] = inner * keep
-                    place = 12 * level + 4 * f + 2 * par
-                    packed = jnp.where(lane == place, spread_out(left) * keep, packed)
-                    packed = jnp.where(lane == place + 1, spread_out(right) * keep, packed)
-            line = jnp.sum(packed, axis=0, keepdims=True)
-            win[order, k, 48:56, :] = jnp.where(level == 6, jnp.broadcast_to(line, (LEV, LANES)), 0.0)
-            return carry
-
-        lax.fori_loop(0, rows // 2, slot, 0)
-
-        for e, row in enumerate((ox - 1 - rows * tile, ox + 256 - rows * tile)):
-            inside = (row >= 0) & (row < rows)
-            keep = jnp.where(inside, 1.0, 0.0).astype(F32)
-            r = jnp.clip(row, 0, rows - 1)
+
+def split_parent(pad, thirds, rows, width):
+    def split(k, carry):
+        part = pad[pl.ds(2 * k, 2), :, :].reshape(48, width)
+        for i in range(3):
+            rounded = part.astype(jnp.bfloat16)
+            thirds[i, pl.ds(pl.multiple_of(48 * k, 48), 48), :] = rounded
+            part = part - rounded.astype(F32)
+        return carry
+
+    lax.fori_loop(0, rows // 2, split, 0)
+
+
+def pack_nest(order, box, thirds, picked, extra, win, rows, cols):
+    lane = lane_ids()
+    level = level_ids()
+    tile = tile_number()
+    nest = (order % 2) * 2 + order // 2
+    ox = box[nest, 0]
+    oy = box[nest, 1]
+    from_col = lax.broadcasted_iota(jnp.int32, (cols, 2 * LANES), 0)
+    to_col = lax.broadcasted_iota(jnp.int32, (cols, 2 * LANES), 1)
+    offset = jnp.where(to_col < LANES, to_col, jnp.where(to_col % 2 == 0, -1, LANES))
+    choice = jnp.where(from_col == offset + (oy - cols * section()), 1.0, 0.0).astype(jnp.bfloat16)
+    total = None
+    for i in range(3):
+        product = jnp.dot(thirds[i], choice, preferred_element_type=F32)
+        total = product if total is None else total + product
+    picked[...] = total.reshape(rows, 24, 2 * LANES)
+
+    for k in range(rows // 2):
+        packed = jnp.zeros((LEV, LANES), F32)
+        for par in range(2):
+            r = 2 * k + par
+            foot = rows * tile + r - ox
+            keep = jnp.where((foot >= 0) & (foot < 256), 1.0, 0.0).astype(F32)
             for f in range(3):
-                inner, _, _ = window(r, f)
-                extra[pl.ds(24 * e + 8 * f, 8), :] = inner * keep
-        for k in range(8):
-            win[order, k, 48:54, :] = extra[6 * k : 6 * k + 6, :]
-
-
-def move_kernel(box, win, edge, nest, parent, slots, low, high, rowhalo, colhalo, near, comb, gathered, summed, ready, sends,
-                sem_s, sem_r, sem1_s, sem1_r, semz_s, semz_r, sem2_s, sem2_r):
+                win[order, k, pl.ds(24 * par + 8 * f, 8), :] = picked[r, pl.ds(8 * f, 8), 0:LANES] * keep
+                here = lane // 2 == 6 * level + 2 * f + par
+                packed = jnp.where(here, picked[r, pl.ds(8 * f, 8), LANES : 2 * LANES] * keep, packed)
+        line = jnp.sum(packed, axis=0, keepdims=True)
+        win[order, k, 48:56, :] = jnp.where(level == 6, jnp.broadcast_to(line, (LEV, LANES)), 0.0)
+
+    for e, row in enumerate((ox - 1 - rows * tile, ox + 256 - rows * tile)):
+        for f in range(3):
+            total = jnp.zeros((LEV, LANES), F32)
+            for r in range(rows):
+                total = total + picked[r, pl.ds(8 * f, 8), 0:LANES] * jnp.where(row == r, 1.0, 0.0).astype(F32)
+            extra[pl.ds(24 * e + 8 * f, 8), :] = total
+    for k in range(8):
+        win[order, k, 48:54, :] = extra[6 * k : 6 * k + 6, :]
+
+
+def move_kernel(box, diffusion, wind, conversion, mix, nest, parent, slots, low, high, parent_out, win, edge, near, comb, gathered,
+                summed, ready, sends, rowhalo, colhalo, pad, thirds, picked, extra, coef, result, sem_s, sem_r, sem1_s, sem1_r, semz_s, semz_r,
+                sem2_s, sem2_r, sem_l):
     yl, co, tx, th, tz = (lax.axis_index(a) for a in ("yl", "co", "tx", "th", "tz"))
     mine = tx * 2 + th
     sec = yl * 2 + co
     tile = tx * 16 + th * 8 + tz
     here = dict(yl=yl, co=co, tx=tx, th=th, tz=tz)
+    rows, chan, cols = parent.shape
 
     def tile_at(t):
         return dict(here, tx=t // 16, th=(t // 8) % 2, tz=t % 8)
@@ -146,26 +142,54 @@
     ring = [dict(here, tz=(tz + dz) % 8) for dz in (4, 3, 5, 2, 6, 1, 7)]
     greet = [core, following, before, east, west] + [c[0] for c in cross] + ring
     barrier = pltpu.get_barrier_semaphore()
+    load = pltpu.make_async_copy(parent, pad, sem_l.at[0])
+    load.start()
     for device in greet:
         pl.semaphore_signal(barrier, inc=1, device_id=device, device_id_type=MESH)
+
+    load.wait()
+    split_parent(pad, thirds, rows, cols)
+    pack_edges(pad, edge, rows, cols)
+
+    def pack(order, carry):
+        pack_nest(order, box, thirds, picked, extra, win, rows, cols)
+        return carry
+
+    lax.fori_loop(0, 4, pack, 0)
     pl.semaphore_wait(barrier, len(greet))
 
-    def send(src, dst, s, r, device):
-        copy = pltpu.make_async_remote_copy(src_ref=src, dst_ref=dst, send_sem=s, recv_sem=r, device_id=device, device_id_type=MESH)
+    def make(src, dst, s, r, device):
+        return pltpu.make_async_remote_copy(src_ref=src, dst_ref=dst, send_sem=s, recv_sem=r, device_id=device, device_id_type=MESH)
+
+    def send(*parts):
+        copy = make(*parts)
         copy.start()
         return copy
 
     first = send(win.at[pl.ds((1 - co) * 2, 2)], near, sem_s.at[0], sem_r.at[0], core)
-    rows = nest.shape[1]
-    last = parent.shape[0] - 1
-    halos = [
+    columns = [
         send(edge.at[1], colhalo.at[0], sem_s.at[1], sem_r.at[1], east),
         send(edge.at[0], colhalo.at[1], sem_s.at[2], sem_r.at[2], west),
-        send(nest.at[0, pl.ds(rows - NSTEP, NSTEP)], low, sem_s.at[3], sem_r.at[3], following),
-        send(nest.at[0, pl.ds(0, NSTEP)], high, sem_s.at[4], sem_r.at[4], before),
-        send(parent.at[last], rowhalo.at[0], sem_s.at[5], sem_r.at[5], following),
-        send(parent.at[0], rowhalo.at[1], sem_s.at[6], sem_r.at[6], before),
     ]
+    span = nest.shape[1]
+    onward = [
+        make(parent.at[rows - 1], rowhalo.at[0], sem_s.at[5], sem_r.at[5], following),
+        make(nest.at[0, pl.ds(span - NSTEP, NSTEP)], low, sem_s.at[3], sem_r.at[3], following),
+    ]
+    backward = [
+        make(parent.at[0], rowhalo.at[1], sem_s.at[6], sem_r.at[6], before),
+        make(nest.at[0, pl.ds(0, NSTEP)], high, sem_s.at[4], sem_r.at[4], before),
+    ]
+
+    def start(copies, where):
+        @pl.when(where)
+        def _():
+            for copy in copies:
+                copy.start()
+
+    start(onward, tz != 7)
+    start(backward, tz != 0)
+    fill_coefs(coef, diffusion, wind, conversion, mix)
     first.wait()
 
     def combine(k, carry):
@@ -180,6 +204,34 @@
         to = device["tx"] * 2 + device["th"]
         copies.append(send(comb.at[device["yl"], to], gathered.at[tx, yl, th], sem1_s.at[j], sem1_r.at[j], device))
     gathered[tx, yl, th] = comb[yl, mine]
+
+    have = [jnp.where(c, 1.0, 0.0).astype(F32) for c in (tile > 0, tile < 63, sec > 0, sec < 3)]
+    lane = lane_ids()
+    count = cols // LANES
+
+    def inner(i):
+        return lambda f, q: pad[i, pl.ds(8 * f, 8), pl.ds(LANES * q, LANES)]
+
+    def outer(which):
+        return lambda f, q: rowhalo[which, pl.ds(8 * f, 8), pl.ds(LANES * q, LANES)] * have[which]
+
+    def one_row(i, north, south):
+        def rim(which):
+            return lambda f: spread_out(
+                jnp.sum(jnp.where(lane == i, colhalo[which, pl.ds(8 * f, 8), :], 0.0), axis=1, keepdims=True) * have[2 + which])
+
+        for q, done in advance(coef, count, north, inner(i), south, rim(0), rim(1)):
+            for f in range(3):
+                result[i, pl.ds(8 * f, 8), pl.ds(LANES * q, LANES)] = done[f]
+
+    def middle(i, carry):
+        one_row(i, inner(i - 1), inner(i + 1))
+        return carry
+
+    for copy in columns:
+        copy.wait()
+    lax.fori_loop(1, rows - 1, middle, 0)
+
     for copy in copies:
         copy.wait()
     for h in range(2):
@@ -190,6 +242,14 @@
         summed[tz, h] = total
 
     copies = [send(summed.at[tz], summed.at[tz], semz_s.at[j], semz_r.at[j], device) for j, device in enumerate(ring)]
+    start(onward, tz == 7)
+    start(backward, tz == 0)
+    onward[0].wait()
+    backward[0].wait()
+    one_row(0, outer(0), inner(1))
+    one_row(rows - 1, inner(rows - 2), outer(1))
+    store = pltpu.make_async_copy(result, parent_out, sem_l.at[1])
+    store.start()
     for copy in copies:
         copy.wait()
 
@@ -217,9 +277,10 @@
             copies.append(send(sends.at[j], ready.at[mine], sem2_s.at[j], sem2_r.at[j], device))
             j += 1
     pick(here, ready, mine)
+    onward[1].wait()
+    backward[1].wait()
+    store.wait()
     for copy in copies:
-        copy.wait()
-    for copy in halos:
         copy.wait()
     slots[...] = ready[...]
 
@@ -281,22 +342,31 @@
 
 def advance(coef, count, north, center, south, first, last):
     lane = lane_ids()
-    moved = [[None] * count for _ in range(3)]
-    for f in range(3):
-        tiles = [center(f, q) for q in range(count)]
-        right = [pltpu.roll(t, 1, 1) for t in tiles]
-        left = [pltpu.roll(t, LANES - 1, 1) for t in tiles]
-        for q in range(count):
-            west = jnp.where(lane == 0, first(f) if q == 0 else right[q - 1], right[q])
-            east = jnp.where(lane == LANES - 1, last(f) if q == count - 1 else left[q + 1], left[q])
-            moved[f][q] = (coef[f, 0] * tiles[q] + coef[f, 1] * north(f, q) + coef[f, 2] * (south(f, q) + east)
-                           + coef[f, 3] * west)
+    tile, right, left = {}, {}, {}
+
+    def read(f, q):
+        if (f, q) not in tile:
+            tile[f, q] = center(f, q)
+            right[f, q] = pltpu.roll(tile[f, q], 1, 1)
+            left[f, q] = pltpu.roll(tile[f, q], LANES - 1, 1)
+
     for q in range(count):
-        yield q, physics(coef, moved[0][q], moved[1][q], moved[2][q])
-
-
-def nest_kernel(box, diffusion, wind, conversion, mix, slots, nest, low, high, out, coef, extra, old, new, flat, wide, state_a, state_b,
-                keep, pull):
+        moved = []
+        for f in range(3):
+            read(f, q)
+            if q + 1 < count:
+                read(f, q + 1)
+            west = jnp.where(lane == 0, first(f) if q == 0 else right[f, q - 1], right[f, q])
+            east = jnp.where(lane == LANES - 1, last(f) if q == count - 1 else left[f, q + 1], left[f, q])
+            moved.append(coef[f, 0] * tile[f, q] + coef[f, 1] * north(f, q) + coef[f, 2] * (south(f, q) + east) + coef[f, 3] * west)
+        yield q, physics(coef, *moved)
+
+
+def nest_kernel(box, diffusion, wind, conversion, mix, slots, nest, low, high, parent_step, out, parent_out, coef, extra, old, new, flat,
+                wide, state_a, state_b, keep, pull, passed, sem):
+    take = pltpu.make_async_copy(parent_step, passed, sem.at[0])
+    give = pltpu.make_async_copy(passed, parent_out, sem.at[1])
+    take.start()
     sec = section()
     t = tile_number()
     rows = nest.shape[1]
@@ -361,6 +431,8 @@
         total = product if total is None else total + product
         part = part - rounded.astype(F32)
     wide[...] = total
+    take.wait()
+    give.start()
 
     wide_rows = rows + 2 * NSTEP
     row_id = rows * t - NSTEP + lax.broadcasted_iota(jnp.int32, (wide_rows, 512), 0)
@@ -419,85 +491,50 @@
             return carry
 
         lax.fori_loop(step, wide_rows - step, one_row, 0)
-
-
-def parent_kernel(diffusion, wind, conversion, mix, parent, rowhalo, colhalo, out, coef):
-    sec = section()
-    t = tile_number()
-    rows = parent.shape[0]
-    count = parent.shape[2] // LANES
-    lane = lane_ids()
-    fill_coefs(coef, diffusion, wind, conversion, mix)
-    have_up = jnp.where(t > 0, 1.0, 0.0).astype(F32)
-    have_down = jnp.where(t < 63, 1.0, 0.0).astype(F32)
-    have_left = jnp.where(sec > 0, 1.0, 0.0).astype(F32)
-    have_right = jnp.where(sec < 3, 1.0, 0.0).astype(F32)
-
-    def inner(i):
-        return lambda f, q: parent[i, pl.ds(8 * f, 8), pl.ds(LANES * q, LANES)]
-
-    def outer(side, scale):
-        return lambda f, q: rowhalo[side, pl.ds(8 * f, 8), pl.ds(LANES * q, LANES)] * scale
-
-    def one_row(i, north, south):
-        def edge(side, scale):
-            return lambda f: spread_out(
-                jnp.sum(jnp.where(lane == i, colhalo[side, pl.ds(8 * f, 8), :], 0.0), axis=1, keepdims=True) * scale)
-
-        for q, done in advance(coef, count, north, inner(i), south, edge(0, have_left), edge(1, have_right)):
-            for f in range(3):
-                out[i, pl.ds(8 * f, 8), pl.ds(LANES * q, LANES)] = done[f]
-
-    one_row(0, outer(0, have_up), inner(1))
-
-    def middle(i, carry):
-        one_row(i, inner(i - 1), inner(i + 1))
-        return carry
-
-    lax.fori_loop(1, rows - 1, middle, 0)
-    one_row(rows - 1, inner(rows - 2), outer(1, have_down))
+    give.wait()
 
 
 def body(parent_old, nest_state, diffusion, wind_speed, conversion, vert_mix, nest_box):
     rows, chan, cols = parent_old.shape
     shape = jax.ShapeDtypeStruct
-    win, edge = pl.pallas_call(
-        pack_kernel,
-        out_shape=(shape((4, 8, SLOT, LANES), F32), shape((2, chan, LANES), F32)),
-        in_specs=[smem(), anywhere()],
-        out_specs=(vmem(), vmem()),
-        scratch_shapes=[pltpu.VMEM((rows, chan, cols + 6 * LANES), F32), pltpu.VMEM((48, LANES), F32), pltpu.SemaphoreType.DMA(())],
-        name="pack",
-    )(nest_box, parent_old)
     dma = pltpu.SemaphoreType.DMA
-    slots, low, high, rowhalo, colhalo = pl.pallas_call(
+    slots, low, high, parent_step = pl.pallas_call(
         move_kernel,
         out_shape=(
             shape((8, SLOT, LANES), F32),
             shape((NSTEP, chan, nest_state.shape[3]), F32),
             shape((NSTEP, chan, nest_state.shape[3]), F32),
-            shape((2, chan, cols), F32),
-            shape((2, chan, LANES), F32),
+            shape(parent_old.shape, F32),
         ),
-        in_specs=[smem(), vmem(), vmem(), anywhere(), anywhere()],
-        out_specs=(vmem(), anywhere(), anywhere(), anywhere(), anywhere()),
+        in_specs=[smem()] * 5 + [anywhere()] * 2,
+        out_specs=(vmem(), anywhere(), anywhere(), anywhere()),
         scratch_shapes=[
+            pltpu.VMEM((4, 8, SLOT, LANES), F32),
+            pltpu.VMEM((2, chan, LANES), F32),
             pltpu.VMEM((2, 8, SLOT, LANES), F32),
             pltpu.VMEM((2, 8, SLOT, LANES), F32),
             pltpu.VMEM((4, 2, 2, SLOT, LANES), F32),
             pltpu.VMEM((8, 2, SLOT, LANES), F32),
             pltpu.VMEM((8, SLOT, LANES), F32),
             pltpu.VMEM((7, SLOT, LANES), F32),
-            dma((7,)), dma((7,)), dma((15,)), dma((15,)), dma((7,)), dma((7,)), dma((7,)), dma((7,)),
+            pltpu.VMEM((2, chan, cols), F32),
+            pltpu.VMEM((2, chan, LANES), F32),
+            pltpu.VMEM((rows, chan, cols), F32),
+            pltpu.VMEM((3, rows * chan, cols), jnp.bfloat16),
+            pltpu.VMEM((rows, chan, 2 * LANES), F32),
+            pltpu.VMEM((48, LANES), F32),
+            pltpu.VMEM((3, 13, LEV, LANES), F32),
+            pltpu.VMEM((rows, chan, cols), F32),
+            dma((7,)), dma((7,)), dma((15,)), dma((15,)), dma((7,)), dma((7,)), dma((7,)), dma((7,)), dma((2,)),
         ],
         compiler_params=pltpu.CompilerParams(collective_id=0, has_side_effects=True),
         name="move",
-    )(nest_box, win, edge, nest_state, parent_old)
-    nest_new = pl.pallas_call(
+    )(nest_box, diffusion, wind_speed, conversion, vert_mix, nest_state, parent_old)
+    nest_new, parent_new = pl.pallas_call(
         nest_kernel,
-        out_shape=shape(nest_state.shape, F32),
-        in_specs=[smem()] * 5 + [vmem()] * 4,
-        out_specs=vmem(),
+        out_shape=(shape(nest_state.shape, F32), shape(parent_old.shape, F32)),
+        in_specs=[smem()] * 5 + [vmem()] * 4 + [anywhere()],
+        out_specs=(vmem(), anywhere()),
         scratch_shapes=[
             pltpu.VMEM((3, 13, LEV, LANES), F32),
             pltpu.VMEM((48, LANES), F32),
@@ -509,17 +546,11 @@
             pltpu.VMEM((24, chan, 512), F32),
             pltpu.VMEM((24, LEV, 512), F32),
             pltpu.VMEM((24, LEV, 512), F32),
+            pltpu.VMEM((rows, chan, cols), F32),
+            dma((2,)),
         ],
         name="nest",
-    )(nest_box, diffusion, wind_speed, conversion, vert_mix, slots, nest_state, low, high)
-    parent_new = pl.pallas_call(
-        parent_kernel,
-        out_shape=shape(parent_old.shape, F32),
-        in_specs=[smem()] * 4 + [vmem()] * 3,
-        out_specs=vmem(),
-        scratch_shapes=[pltpu.VMEM((3, 13, LEV, LANES), F32)],
-        name="parent",
-    )(diffusion, wind_speed, conversion, vert_mix, parent_old, rowhalo, colhalo)
+    )(nest_box, diffusion, wind_speed, conversion, vert_mix, slots, nest_state, low, high, parent_step)
     return parent_new, nest_new
 
 

time: 70.9 us -> 61.7 us (0.87); the launches traced: 69.9 us -> 61.5 us
  Pallas kernels: 69.3 us -> 60.9 us
    pallas_call x3 -> x1, Pallas kernels: 28 us -> 13.6 us  [body(): pl.pallas_call(nest_kernel, out_shape=(shape(nest_state.shape, F32), shap...]
    pallas_call x1, Pallas kernels: 41.3 us -> 47.3 us  [body(): pl.pallas_call(move_kernel, out_shape=(shape((8, SLOT, LANES), F32), shap...]
where the time goes in v2:
time: 61.7 us; the launch traced here: 61.5 us
  Pallas kernels  60.9 us (99%)
  between operations  0.64 us (1%)
    pallas_call x1, Pallas kernels, body(): pl.pallas_call(move_kernel, out_shape=(shape((8, SLOT, LANES), F32), shap...  47.3 us
    pallas_call x1, Pallas kernels, body(): pl.pallas_call(nest_kernel, out_shape=(shape(nest_state.shape, F32), shap...  13.6 us

profile of v2, /device:TPU:1, one launch (start us, length us, event | category | flops | bytes accessed | tf_op | source)
XLA Modules:
  0.0 61.5 jit_solution(14089628890803946140)
XLA Ops:
  0.6 47.3 %move.1 = (f32[8,56,128]{2,1,0:T(8,128)}, f32[4,24,512]{2,1,0:T(8,128)}, f32[4,24,512]{2,1,0:T(8,128)}, f32[16,24,1024]{2,1,0:T(8,128)}) custom-call(s32[4,4]{1,0:T(4,128)} %box.3, f32[24]{0:T(128)} %diffusion.3, f32[2,24]{1,0:T(2,128)} %wind.3, f32[2,8]{1,0:T(2,128)} %conversion.3, f32[3]{0:T(128)} %mix.3, f32[1,16,24,512]{3,2,1,0:T(8,128)} %nest.5, ...), custom_call_target="tpu_custom_call" | custom-call | tf_op jit(solution)/shard_map/move/pallas_call | solution.py:501
  48.0 13.6 %nest.4 = (f32[1,16,24,512]{3,2,1,0:T(8,128)}, f32[16,24,1024]{2,1,0:T(8,128)}) custom-call(s32[4,4]{1,0:T(4,128)} %box.3, f32[24]{0:T(128)} %diffusion.3, f32[2,24]{1,0:T(2,128)} %wind.3, f32[2,8]{1,0:T(2,128)} %conversion.3, f32[3]{0:T(128)} %mix.3, f32[8,56,128]{2,1,0:T(8,128)} %get-tuple-element.8.slots, f32[1,16,24,512]{3,2,1,0:T(8,128)} %nest.5, ...), custom_call_target="tpu_custom_call" | custom-call | tf_op jit(solution)/shard_map/nest/pallas_call | solution.py:533

commit v3 on v2

v3 whole, which is shorter than its diff:
```python
import itertools

import jax
import jax.numpy as jnp
from jax import lax
from jax.experimental import pallas as pl
from jax.experimental.pallas import tpu as pltpu
from jax.sharding import Mesh
from jax.sharding import PartitionSpec as P

NSTEP = 4
LEV = 8
SEC = ("yl", "co")
TILE = ("tx", "th", "tz")
LANES = 128
SLOT = (7, 8, 128)
APRON = 2
MESH = pl.DeviceIdType.MESH
F32 = jnp.float32


def vmem():
    return pl.BlockSpec(memory_space=pltpu.VMEM)


def smem():
    return pl.BlockSpec(memory_space=pltpu.SMEM)


def anywhere():
    return pl.BlockSpec(memory_space=pl.ANY)


def section():
    return lax.axis_index("yl") * 2 + lax.axis_index("co")


def tile_number():
    return lax.axis_index("tx") * 16 + lax.axis_index("th") * 8 + lax.axis_index("tz")


def lane_ids():
    return lax.broadcasted_iota(jnp.int32, (LEV, LANES), 1)


def level_ids():
    return lax.broadcasted_iota(jnp.int32, (LEV, LANES), 0)


def spread_out(column):
    return jnp.broadcast_to(column, (LEV, LANES))


def pack_edges(pad, edge, rows, count):
    lane = lane_ids()
    for which in range(2):
        block, off = (APRON, 0) if which == 0 else (APRON + count - 1, LANES - 1)
        for f in range(3):
            total = jnp.zeros((LEV, LANES), F32)
            for r in range(rows):
                piece = pad[block, r, pl.ds(8 * f, 8), :]
                total = jnp.where(lane == r, spread_out(piece[:, off : off + 1]), total)
            edge[which, pl.ds(8 * f, 8), :] = total


def pack_nest(order, box, pad, extra, win, rows, cols):
    lane = lane_ids()
    level = level_ids()
    tile = tile_number()
    nest = (order % 2) * 2 + order // 2
    ox = box[nest, 0]
    oy = box[nest, 1]
    start = jnp.clip(oy - cols * section() - 1, -APRON * LANES, cols) + APRON * LANES
    block = start // LANES
    shift = start - block * LANES + 1

    back = (LANES - shift) % LANES

    def turned(piece):
        return pltpu.roll(piece, back, 1)

    def window(r, f):
        near = turned(pad[block, r, pl.ds(8 * f, 8), :])
        next_piece = pad[block + 1, r, pl.ds(8 * f, 8), :]
        far = turned(next_piece)
        return jnp.where(lane + shift < LANES, near, far), near, far

    for k in range(rows // 2):
        packed = jnp.zeros((LEV, LANES), F32)
        for par in range(2):
            r = 2 * k + par
            foot = rows * tile + r - ox
            keep = jnp.where((foot >= 0) & (foot < 256), 1.0, 0.0).astype(F32)
            for f in range(3):
                inner, near, far = window(r, f)
                win[order, k, 3 * par + f] = inner * keep
                far = jnp.where(shift < LANES, far, pad[block + 2, r, pl.ds(8 * f, 8), :])
                pair = jnp.where(lane % 2 == 0, spread_out(near[:, LANES - 1 : LANES]), spread_out(far[:, 0:1]))
                packed = jnp.where(lane // 2 == 6 * level + 2 * f + par, pair * keep, packed)
        line = jnp.sum(packed, axis=0, keepdims=True)
        win[order, k, 6] = jnp.where(level == 6, jnp.broadcast_to(line, (LEV, LANES)), 0.0)

    for e, row in enumerate((ox - 1 - rows * tile, ox + 256 - rows * tile)):
        keep = jnp.where((row >= 0) & (row < rows), 1.0, 0.0).astype(F32)
        r = jnp.clip(row, 0, rows - 1)
        for f in range(3):
            extra[pl.ds(24 * e + 8 * f, 8), :] = window(r, f)[0] * keep
    for k in range(8):
        win[order, k, 6, 0:6, :] = extra[6 * k : 6 * k + 6, :]


def step_kernel(box, diffusion, wind, conversion, mix, nest, parent, parent_out, nest_out, win, edge, near, comb, gathered, summed,
                ready, sends, rowhalo, colhalo, pad, extra, coef, result, own, low, high, state_a, state_b, keep, pull, mixer, old, new,
                flat, wide, base, drift, sem_s, sem_r, sem1_s, sem1_r, semz_s, semz_r, sem2_s, sem2_r, sem_p, sem_l):
    yl, co, tx, th, tz = (lax.axis_index(a) for a in ("yl", "co", "tx", "th", "tz"))
    mine = tx * 2 + th
    sec = yl * 2 + co
    tile = tx * 16 + th * 8 + tz
    here = dict(yl=yl, co=co, tx=tx, th=th, tz=tz)
    rows, chan, cols = parent.shape
    count = cols // LANES
    span, width = nest.shape[1], nest.shape[3]
    tall = span + 2 * NSTEP
    lane = lane_ids()
    level = level_ids()

    def tile_at(t):
        return dict(here, tx=t // 16, th=(t // 8) % 2, tz=t % 8)

    def sec_at(s):
        return dict(here, yl=s // 2, co=s % 2)

    core = dict(here, co=1 - co)
    following, before = tile_at((tile + 1) % 64), tile_at((tile + 63) % 64)
    east, west = sec_at((sec + 1) % 4), sec_at((sec + 3) % 4)
    cross = [
        (dict(here, tx=(tx + dx) % 4, th=(th + dh) % 2, yl=(yl + dl) % 2), dx, dh, dl)
        for dx, dh, dl in itertools.product((2, 1, 3, 0), (1, 0), (1, 0))
        if (dx, dh, dl) != (0, 0, 0)
    ]
    ring = [dict(here, tz=(tz + dz) % 8) for dz in (4, 3, 5, 2, 6, 1, 7)]
    greet = [core, following, before, east, west] + [c[0] for c in cross] + ring
    barrier = pltpu.get_barrier_semaphore()
    loads = [
        pltpu.make_async_copy(parent.at[:, :, pl.ds(LANES * q, LANES)], pad.at[APRON + q], sem_p.at[q]) for q in range(count)
    ]
    for copy in loads:
        copy.start()
    load_own = pltpu.make_async_copy(nest.at[0], own, sem_l.at[0])
    load_own.start()
    for device in greet:
        pl.semaphore_signal(barrier, inc=1, device_id=device, device_id_type=MESH)

    def empty(i, carry):
        for q in (0, 1, APRON + count, APRON + count + 1, APRON + count + 2):
            pad[q, i] = jnp.zeros((chan, LANES), F32)
        return carry

    lax.fori_loop(0, rows, empty, 0)
    for copy in loads:
        copy.wait()

    def pack(order, carry):
        pack_nest(order, box, pad, extra, win, rows, cols)
        return carry

    lax.fori_loop(0, 4, pack, 0)
    pl.semaphore_wait(barrier, len(greet))

    def make(src, dst, s, r, device):
        return pltpu.make_async_remote_copy(src_ref=src, dst_ref=dst, send_sem=s, recv_sem=r, device_id=device, device_id_type=MESH)

    def send(*parts):
        copy = make(*parts)
        copy.start()
        return copy

    first = send(win.at[pl.ds((1 - co) * 2, 2)], near, sem_s.at[0], sem_r.at[0], core)
    onward = [
        make(parent.at[rows - 1], rowhalo.at[0], sem_s.at[5], sem_r.at[5], following),
        make(nest.at[0, pl.ds(span - NSTEP, NSTEP)], low, sem_s.at[3], sem_r.at[3], following),
    ]
    backward = [
        make(parent.at[0], rowhalo.at[1], sem_s.at[6], sem_r.at[6], before),
        make(nest.at[0, pl.ds(0, NSTEP)], high, sem_s.at[4], sem_r.at[4], before),
    ]

    def start(copies, where):
        @pl.when(where)
        def _():
            for copy in copies:
                copy.start()

    start(onward, tz != 7)
    start(backward, tz != 0)
    pack_edges(pad, edge, rows, count)
    columns = [
        send(edge.at[1], colhalo.at[0], sem_s.at[1], sem_r.at[1], east),
        send(edge.at[0], colhalo.at[1], sem_s.at[2], sem_r.at[2], west),
    ]
    fill_coefs(coef, diffusion, wind, conversion, mix)
    first.wait()

    def combine(k, carry):
        for l in range(2):
            comb[l, k] = win[co * 2 + l, k] + near[l, k]
        return carry

    lax.fori_loop(0, 8, combine, 0)

    copies = []
    for j, (device, dx, dh, dl) in enumerate(cross):
        to = device["tx"] * 2 + device["th"]
        copies.append(send(comb.at[device["yl"], to], gathered.at[tx, yl, th], sem1_s.at[j], sem1_r.at[j], device))
    gathered[tx, yl, th] = comb[yl, mine]

    have = [jnp.where(c, 1.0, 0.0).astype(F32) for c in (tile > 0, tile < 63, sec > 0, sec < 3)]

    def inner(i):
        return lambda f, q: pad[APRON + q, i, pl.ds(8 * f, 8), :]

    def outer(which):
        return lambda f, q: rowhalo[which, pl.ds(8 * f, 8), pl.ds(LANES * q, LANES)] * have[which]

    def parent_row(i, north, south):
        def rim(which):
            return lambda f: spread_out(
                jnp.sum(jnp.where(lane == i, colhalo[which, pl.ds(8 * f, 8), :], 0.0), axis=1, keepdims=True) * have[2 + which])

        for q, done in advance(coef, count, north, inner(i), south, rim(0), rim(1)):
            for f in range(3):
                result[i, pl.ds(8 * f, 8), pl.ds(LANES * q, LANES)] = done[f]

    def parent_rows(i, carry):
        parent_row(i, inner(i - 1), inner(i + 1))
        return carry

    for copy in columns:
        copy.wait()
    lax.fori_loop(1, rows - 1, parent_rows, 0)

    ox, ex, ey = box[sec, 0], box[sec, 2], box[sec, 3]
    row_id = span * tile - NSTEP + lax.broadcasted_iota(jnp.int32, (tall, width), 0)
    col_id = lax.broadcasted_iota(jnp.int32, (tall, width), 1)
    live = jnp.where((row_id >= 0) & (row_id < ex) & (col_id < ey), 1.0, 0.0).astype(F32)
    distance = jnp.minimum(jnp.minimum(row_id, col_id), jnp.minimum(ex - 1 - row_id, ey - 1 - col_id))
    nudging = 0.1 + 0.4 * jnp.exp(jnp.maximum(distance, 0).astype(F32) * (-1.0 / 3.0))
    kept, pulled = live * (1.0 - nudging), live * nudging
    for i in range(tall):
        keep[i] = jnp.broadcast_to(kept[i : i + 1, :], (LEV, width))
        pull[i] = jnp.broadcast_to(pulled[i : i + 1, :], (LEV, width))

    def begin(src, i, at):
        number = span * tile - NSTEP + at
        alive = jnp.where((number >= 0) & (number < ex) & (lax.broadcasted_iota(jnp.int32, (chan, width), 1) < ey), 1.0, 0.0)
        state_a[at] = src[i] * alive.astype(F32)

    def begin_own(i, carry):
        begin(own, i, NSTEP + i)
        return carry

    load_own.wait()
    lax.fori_loop(0, span, begin_own, 0)
    zero = jnp.zeros((LEV, LANES), F32)
    blocks = width // LANES

    def nest_row(src, i):
        read = lambda k: lambda f, q: src[k, pl.ds(8 * f, 8), pl.ds(LANES * q, LANES)]
        yield from advance(coef, blocks, read(i - 1), read(i), read(i + 1), lambda f: zero, lambda f: zero)

    def first_row(i):
        for q, done in nest_row(state_a, i):
            for f in range(3):
                state_b[i, pl.ds(8 * f, 8), pl.ds(LANES * q, LANES)] = done[f]

    def first_rows(first):
        def pair(m, carry):
            first_row(first + 2 * m)
            first_row(first + 2 * m + 1)
            return carry

        return pair

    lax.fori_loop(0, span // 2 - 1, first_rows(NSTEP + 1), 0)

    cells = lax.broadcasted_iota(jnp.int32, (LANES, width), 0)
    targets = lax.broadcasted_iota(jnp.int32, (LANES, width), 1)
    weight = (targets % 4).astype(F32) * 0.25
    low_cell = targets // 4
    high_cell = jnp.minimum(low_cell + 1, LANES - 1)
    mixed = (jnp.where(cells == low_cell, 1.0 - weight, 0.0) + jnp.where(cells == high_cell, weight, 0.0)).astype(jnp.bfloat16)
    for i in range(3):
        mixer[LANES * i : LANES * (i + 1), :] = mixed

    for copy in copies:
        copy.wait()
    for h in range(2):
        total = gathered[0, 0, h]
        for x, l in itertools.product(range(4), range(2)):
            if (x, l) != (0, 0):
                total = total + gathered[x, l, h]
        summed[tz, h] = total

    copies = [send(summed.at[tz], summed.at[tz], semz_s.at[j], semz_r.at[j], device) for j, device in enumerate(ring)]
    start(onward, tz == 7)
    start(backward, tz == 0)

    onward[0].wait()
    backward[0].wait()
    parent_row(0, outer(0), inner(1))
    parent_row(rows - 1, inner(rows - 2), outer(1))
    store = pltpu.make_async_copy(result, parent_out, sem_l.at[1])
    store.start()
    onward[1].wait()
    backward[1].wait()
    for i in range(NSTEP):
        begin(low, i, i)
        begin(high, i, span + NSTEP + i)
    lax.fori_loop(0, 2, first_rows(1), 0)
    lax.fori_loop(0, 2, first_rows(span + NSTEP - 1), 0)
    for copy in copies:
        copy.wait()

    lines = summed[0, 0, 6]
    for z, h in itertools.product(range(8), range(2)):
        if (z, h) != (0, 0):
            lines = lines + summed[z, h, 6]

    def pick(device, where, slot):
        t = device["tx"] * 16 + device["th"] * 8 + tz
        q = ((ox + 4 * t + 254) % 256) // 2
        q = (q + (mine - q + 128) % 8) % 128
        z, h = (q // 8) % 8, q // 64
        where[slot, 0:6] = summed[z, h, 0:6]
        where[slot, 6] = jnp.where(level < 6, lines, summed[z, h, 6])

    copies = []
    j = 0
    for device, dx, dh, dl in cross:
        if dl == 0:
            pick(device, sends, j)
            copies.append(send(sends.at[j], ready.at[mine], sem2_s.at[j], sem2_r.at[j], device))
            j += 1
    pick(here, ready, mine)
    store.wait()
    for copy in copies:
        copy.wait()

    for k in range(8):
        extra[6 * k : 6 * k + 6, :] = ready[k, 6, 0:6, :]

    def place(j):
        residue = (ox + 4 * tile + 254 + j) % 256
        return (residue // 2) % 8, residue % 2

    for j in range(9):
        k, par = place(j)
        for f in range(3):
            old[j, pl.ds(8 * f, 8), :] = ready[k, 3 * par + f]

    @pl.when(tile == 0)
    def _():
        old[1] = extra[0:24, :]

    @pl.when(tile == 63)
    def _():
        old[6] = extra[24:48, :]

    for j in range(1, 8):
        k, par = place(j)
        line = jnp.broadcast_to(ready[k, 6][6:7, :], (LEV, LANES))

        def beyond(which):
            def column(f):
                at = 12 * level + 4 * f + 2 * par + which
                return spread_out(jnp.sum(jnp.where(lane == at, line, 0.0), axis=1, keepdims=True))

            return column

        read = lambda i: lambda f, q: old[i, pl.ds(8 * f, 8), :]
        for q, done in advance(coef, 1, read(j - 1), read(j), read(j + 1), beyond(0), beyond(1)):
            for f in range(3):
                new[j - 1, pl.ds(8 * f, 8), :] = done[f]

    @pl.when(tile == 63)
    def _():
        old[6] = old[5]
        new[5] = new[4]

    for j in range(7):
        part = jnp.concatenate([old[j + 1], (new[j] - old[j + 1]) * (1.0 / NSTEP)], axis=0)
        for i in range(3):
            rounded = part.astype(jnp.bfloat16)
            flat[pl.ds(48 * j, 48), LANES * i : LANES * (i + 1)] = rounded
            part = part - rounded.astype(F32)
    wide[...] = jnp.dot(flat[...], mixer[...], preferred_element_type=F32).reshape(7, 2 * chan, width)

    def pulls(u, carry):
        for q in range(blocks):
            columns = pl.ds(LANES * q, LANES)
            for f in range(3):
                at, to = pl.ds(8 * f, 8), pl.ds(chan + 8 * f, 8)
                from_old, from_change = wide[u, at, columns], wide[u, to, columns]
                over_old, over_change = wide[u + 1, at, columns] - from_old, wide[u + 1, to, columns] - from_change
                for p in range(4):
                    i = 4 * u + p
                    p_row = pull[i, :, columns]
                    now, change = (from_old, from_change) if p == 0 else (from_old + 0.25 * p * over_old, from_change + 0.25 * p * over_change)
                    now, change = p_row * now, p_row * change
                    base[i, at, columns] = now
                    drift[i, at, columns] = change
                    state_b[i, at, columns] = keep[i, :, columns] * state_b[i, at, columns] + (now + change)
        return carry

    state_b[0] = jnp.zeros((chan, width), F32)
    state_b[tall - 1] = jnp.zeros((chan, width), F32)
    lax.fori_loop(0, tall // 4, pulls, 0)

    def step_pairs(src, dst, step, first):
        def pair(m, carry):
            for i in (first + 2 * m, first + 2 * m + 1):
                for q, done in nest_row(src, i):
                    columns = pl.ds(LANES * q, LANES)
                    k_row = keep[i, :, columns]
                    for f in range(3):
                        at = pl.ds(8 * f, 8)
                        dst[i, at, columns] = k_row * done[f] + (base[i, at, columns] + float(step) * drift[i, at, columns])
            return carry

        return pair

    lax.fori_loop(0, (tall - 4) // 2, step_pairs(state_b, state_a, 2, 2), 0)
    lax.fori_loop(0, (tall - 6) // 2, step_pairs(state_a, state_b, 3, 3), 0)
    half = span // 2
    parts = []
    for part in range(2):
        lax.fori_loop(0, half // 2, step_pairs(state_b, state_a, 4, NSTEP + half * part), 0)
        parts.append(pltpu.make_async_copy(state_a.at[pl.ds(NSTEP + half * part, half)], nest_out.at[0, pl.ds(half * part, half)], sem_l.at[2 + part]))
        parts[-1].start()
    for copy in parts:
        copy.wait()


def fill_coefs(coef, diffusion, wind, conversion, mix):
    level = level_ids()

    def column(read):
        out = jnp.zeros((LEV, LANES), F32)
        for l in range(LEV):
            out = jnp.where(level == l, read(l), out)
        return out

    for f in range(3):
        d = column(lambda l: diffusion[8 * f + l])
        wx = column(lambda l: wind[0, 8 * f + l])
        wy = column(lambda l: wind[1, 8 * f + l])
        coef[f, 0] = 1.0 - 4.0 * d - wx - wy
        coef[f, 1] = d + wx
        coef[f, 2] = d
        coef[f, 3] = d + wy
        m = mix[f] * jnp.ones((LEV, LANES), F32)
        lower = jnp.where(level > 0, -m, 0.0)
        upper = jnp.where(level < LEV - 1, -m, 0.0)
        diag = 1.0 + m * jnp.where((level == 0) | (level == LEV - 1), 1.0, 2.0)
        item = 7
        for s in (1, 2, 4):
            alpha = -lower / pltpu.roll(diag, s, 0)
            gamma = -upper / pltpu.roll(diag, LEV - s, 0)
            new_diag = diag + alpha * pltpu.roll(upper, s, 0) + gamma * pltpu.roll(lower, LEV - s, 0)
            lower, upper = alpha * pltpu.roll(lower, s, 0), gamma * pltpu.roll(upper, LEV - s, 0)
            diag = new_diag
            if s < 4:
                coef[f, item] = alpha
                coef[f, item + 1] = gamma
                item += 2
            else:
                coef[f, item] = 1.0 / diag
                coef[f, item + 1] = (alpha + gamma) / diag
    c0 = column(lambda l: conversion[0, l])
    c1 = column(lambda l: conversion[1, l])
    coef[0, 4] = c0
    coef[0, 5] = 1.0 - c0
    coef[1, 4] = c1
    coef[1, 5] = 1.0 - c1


def solve(coef, f, r):
    r = r + coef[f, 7] * pltpu.roll(r, 1, 0) + coef[f, 8] * pltpu.roll(r, 7, 0)
    r = r + coef[f, 9] * pltpu.roll(r, 2, 0) + coef[f, 10] * pltpu.roll(r, 6, 0)
    return coef[f, 11] * r + coef[f, 12] * pltpu.roll(r, 4, 0)


def physics(coef, vapour, cloud, rain):
    wet = cloud + coef[0, 4] * vapour
    fields = (coef[0, 5] * vapour, coef[1, 5] * wet, rain + coef[1, 4] * wet)
    return [solve(coef, f, fields[f]) for f in range(3)]


def advance(coef, count, north, center, south, first, last):
    lane = lane_ids()
    tile, right, left = {}, {}, {}

    def read(f, q):
        if (f, q) not in tile:
            tile[f, q] = center(f, q)
            right[f, q] = pltpu.roll(tile[f, q], 1, 1)
            left[f, q] = pltpu.roll(tile[f, q], LANES - 1, 1)

    for q in range(count):
        moved = []
        for f in range(3):
            read(f, q)
            if q + 1 < count:
                read(f, q + 1)
            west = jnp.where(lane == 0, first(f) if q == 0 else right[f, q - 1], right[f, q])
            east = jnp.where(lane == LANES - 1, last(f) if q == count - 1 else left[f, q + 1], left[f, q])
            moved.append(coef[f, 0] * tile[f, q] + coef[f, 1] * north(f, q) + coef[f, 2] * (south(f, q) + east) + coef[f, 3] * west)
        yield q, physics(coef, *moved)


def body(parent_old, nest_state, diffusion, wind_speed, conversion, vert_mix, nest_box):
    rows, chan, cols = parent_old.shape
    span, width = nest_state.shape[1], nest_state.shape[3]
    tall = span + 2 * NSTEP
    shape = jax.ShapeDtypeStruct
    dma = pltpu.SemaphoreType.DMA

    def room(*dims, kind=F32):
        return pltpu.VMEM(dims, kind)

    return pl.pallas_call(
        step_kernel,
        out_shape=(shape(parent_old.shape, F32), shape(nest_state.shape, F32)),
        in_specs=[smem()] * 5 + [anywhere()] * 2,
        out_specs=(anywhere(), anywhere()),
        scratch_shapes=[
            room(4, 8, *SLOT), room(2, chan, LANES), room(2, 8, *SLOT), room(2, 8, *SLOT), room(4, 2, 2, *SLOT), room(8, 2, *SLOT),
            room(8, *SLOT), room(7, *SLOT), room(2, chan, cols), room(2, chan, LANES),
            room(cols // LANES + 5, rows, chan, LANES), room(48, LANES), room(3, 13, LEV, LANES), room(rows, chan, cols),
            room(span, chan, width), room(NSTEP, chan, width), room(NSTEP, chan, width), room(tall, chan, width), room(tall, chan, width),
            room(tall, LEV, width), room(tall, LEV, width), room(3 * LANES, width, kind=jnp.bfloat16),
            room(9, chan, LANES), room(7, chan, LANES), room(14 * chan, 3 * LANES, kind=jnp.bfloat16), room(7, 2 * chan, width),
            room(tall, chan, width), room(tall, chan, width),
            dma((7,)), dma((7,)), dma((15,)), dma((15,)), dma((7,)), dma((7,)), dma((7,)), dma((7,)), dma((cols // LANES,)), dma((4,)),
        ],
        compiler_params=pltpu.CompilerParams(collective_id=0, has_side_effects=True),
        name="step",
    )(nest_box, diffusion, wind_speed, conversion, vert_mix, nest_state, parent_old)


def solution(mesh):
    grid = Mesh(mesh.devices.reshape(2, 2, 4, 2, 8), SEC + TILE)
    in_specs = (P(TILE, None, SEC), P(SEC, TILE, None, None), P(), P(), P(), P(), P())
    out_specs = (P(TILE, None, SEC), P(SEC, TILE, None, None))
    return jax.shard_map(body, mesh=grid, in_specs=in_specs, out_specs=out_specs, check_vma=False)
```

time: 61.7 us -> 63.1 us (1.023)
  local copies, waits for them, and re-layouts: 0 us -> 3.68 us
  Pallas kernels: 60.9 us -> 58.6 us
    unnamed x0 -> x4, local copies, waits for them, and re-layouts: none -> 3.68 us
    pallas_call x2 -> x1, Pallas kernels: 60.9 us -> 58.6 us  [body(): pl.pallas_call(step_kernel, out_shape=(shape(parent_old.shape, F32), shap...]
where the time goes in v3:
time: 63.1 us; the launch traced here: 62.9 us
  Pallas kernels  58.6 us (93%)
  local copies, waits for them, and re-layouts  3.68 us (6%)
  between operations  0.65 us (1%)
    pallas_call x1, Pallas kernels, body(): pl.pallas_call(step_kernel, out_shape=(shape(parent_old.shape, F32), shap...  58.6 us
    unnamed x4, local copies, waits for them, and re-layouts  3.68 us

profile of v3, /device:TPU:1, one launch (start us, length us, event | category | flops | bytes accessed | tf_op | source)
XLA Modules:
  0.0 62.9 jit_solution(1715783628997243409)
XLA Ops:
  0.6 58.6 %step.1 = (f32[16,24,1024]{2,1,0:T(8,128)}, f32[1,16,24,512]{3,2,1,0:T(8,128)}) custom-call(s32[4,4]{1,0:T(4,128)} %box.1, f32[24]{0:T(128)} %diffusion.1, f32[2,24]{1,0:T(2,128)} %wind.1, f32[2,8]{1,0:T(2,128)} %conversion.1, f32[3]{0:T(128)} %mix.1, f32[1,16,24,512]{3,2,1,0:T(8,128)} %nest.1, f32[16,24,1024]{2,1,0:T(8,128)} %parent.1), custom_call_target="tpu_custom_call" | custom-call | tf_op jit(solution)/shard_map/step/pallas_call | solution.py:531
  59.2 0.0 copy-start
  59.2 2.8 %copy.11 = f32[16,24,1024]{2,1,0:T(8,128)} copy(f32[16,24,1024]{2,1,0:T(8,128)} %get-tuple-element.4) | data formatting | bytes 3145728
  62.0 0.0 copy-done
  62.0 0.9 %copy.12 = f32[1,16,24,512]{3,2,1,0:T(8,128)} copy(f32[1,16,24,512]{3,2,1,0:T(8,128)S(1)} %copy-done) | data formatting | bytes 1572864
Async XLA Ops:
  59.2 2.8 %copy-start = (f32[1,16,24,512]{3,2,1,0:T(8,128)S(1)}, f32[1,16,24,512]{3,2,1,0:T(8,128)}, u32[]{:S(2)}) copy-start(f32[1,16,24,512]{3,2,1,0:T(8,128)} %get-tuple-element.5) | copy-start | bytes 2359300

commit v4 on v3

--- a/solution.py
+++ b/solution.py
@@ -109,9 +109,10 @@
         win[order, k, 6, 0:6, :] = extra[6 * k : 6 * k + 6, :]
 
 
-def step_kernel(box, diffusion, wind, conversion, mix, nest, parent, parent_out, nest_out, win, edge, near, comb, gathered, summed,
-                ready, sends, rowhalo, colhalo, pad, extra, coef, result, own, low, high, state_a, state_b, keep, pull, mixer, old, new,
-                flat, wide, base, drift, sem_s, sem_r, sem1_s, sem1_r, semz_s, semz_r, sem2_s, sem2_r, sem_p, sem_l):
+def step_kernel(box, diffusion, wind, conversion, mix, nest, parent, parent_out, slots_out, moved_out, keep_out, pull_out, mixer_out,
+                coef_out, win, edge, near, comb, gathered, summed,
+                ready, sends, rowhalo, colhalo, pad, extra, coef, result, own, low, high, state_a, state_b, keep, pull, mixer,
+                sem_s, sem_r, sem1_s, sem1_r, semz_s, semz_r, sem2_s, sem2_r, sem_p, sem_l):
     yl, co, tx, th, tz = (lax.axis_index(a) for a in ("yl", "co", "tx", "th", "tz"))
     mine = tx * 2 + th
     sec = yl * 2 + co
@@ -164,7 +165,7 @@
         pack_nest(order, box, pad, extra, win, rows, cols)
         return carry
 
-    lax.fori_loop(0, 4, pack, 0)
+    lax.fori_loop((1 - co) * 2, (1 - co) * 2 + 2, pack, 0)
     pl.semaphore_wait(barrier, len(greet))
 
     def make(src, dst, s, r, device):
@@ -185,14 +186,9 @@
         make(nest.at[0, pl.ds(0, NSTEP)], high, sem_s.at[4], sem_r.at[4], before),
     ]
 
-    def start(copies, where):
-        @pl.when(where)
-        def _():
-            for copy in copies:
-                copy.start()
-
-    start(onward, tz != 7)
-    start(backward, tz != 0)
+    for copy in onward + backward:
+        copy.start()
+    lax.fori_loop(co * 2, co * 2 + 2, pack, 0)
     pack_edges(pad, edge, rows, count)
     columns = [
         send(edge.at[1], colhalo.at[0], sem_s.at[1], sem_r.at[1], east),
@@ -261,15 +257,9 @@
 
     load_own.wait()
     lax.fori_loop(0, span, begin_own, 0)
-    zero = jnp.zeros((LEV, LANES), F32)
-    blocks = width // LANES
-
-    def nest_row(src, i):
-        read = lambda k: lambda f, q: src[k, pl.ds(8 * f, 8), pl.ds(LANES * q, LANES)]
-        yield from advance(coef, blocks, read(i - 1), read(i), read(i + 1), lambda f: zero, lambda f: zero)
 
     def first_row(i):
-        for q, done in nest_row(state_a, i):
+        for q, done in nest_row(coef, state_a, i):
             for f in range(3):
                 state_b[i, pl.ds(8 * f, 8), pl.ds(LANES * q, LANES)] = done[f]
 
@@ -302,13 +292,47 @@
         summed[tz, h] = total
 
     copies = [send(summed.at[tz], summed.at[tz], semz_s.at[j], semz_r.at[j], device) for j, device in enumerate(ring)]
-    start(onward, tz == 7)
-    start(backward, tz == 0)
+    out_moved, out_keep, out_pull = (
+        pltpu.make_async_copy(src, dst, sem_l.at[i])
+        for i, (src, dst) in enumerate(((state_b, moved_out), (keep, keep_out), (pull, pull_out)), 2)
+    )
+    out_keep.start()
+    out_pull.start()
+    out_mixer = pltpu.make_async_copy(mixer, mixer_out, sem_l.at[5])
+    out_mixer.start()
+    out_coef = pltpu.make_async_copy(coef, coef_out, sem_l.at[6])
+    out_coef.start()
+    for copy in copies:
+        copy.wait()
+
+    lines = summed[0, 0, 6]
+    for z, h in itertools.product(range(8), range(2)):
+        if (z, h) != (0, 0):
+            lines = lines + summed[z, h, 6]
+
+    def pick(device, where, slot):
+        t = device["tx"] * 16 + device["th"] * 8 + tz
+        q = ((ox + 4 * t + 254) % 256) // 2
+        q = (q + (mine - q + 128) % 8) % 128
+        z, h = (q // 8) % 8, q // 64
+        where[slot, 0:6] = summed[z, h, 0:6]
+        where[slot, 6] = jnp.where(level < 6, lines, summed[z, h, 6])
+
+    copies = []
+    j = 0
+    for device, dx, dh, dl in cross:
+        if dl == 0:
+            pick(device, sends, j)
+            copies.append(send(sends.at[j], ready.at[mine], sem2_s.at[j], sem2_r.at[j], device))
+            j += 1
+    pick(here, ready, mine)
 
     onward[0].wait()
     backward[0].wait()
     parent_row(0, outer(0), inner(1))
     parent_row(rows - 1, inner(rows - 2), outer(1))
+    state_b[0] = jnp.zeros((chan, width), F32)
+    state_b[tall - 1] = jnp.zeros((chan, width), F32)
     store = pltpu.make_async_copy(result, parent_out, sem_l.at[1])
     store.start()
     onward[1].wait()
@@ -318,127 +342,14 @@
         begin(high, i, span + NSTEP + i)
     lax.fori_loop(0, 2, first_rows(1), 0)
     lax.fori_loop(0, 2, first_rows(span + NSTEP - 1), 0)
+    out_moved.start()
+    for copy in (store, out_keep, out_pull, out_mixer, out_coef, out_moved):
+        copy.wait()
     for copy in copies:
         copy.wait()
-
-    lines = summed[0, 0, 6]
-    for z, h in itertools.product(range(8), range(2)):
-        if (z, h) != (0, 0):
-            lines = lines + summed[z, h, 6]
-
-    def pick(device, where, slot):
-        t = device["tx"] * 16 + device["th"] * 8 + tz
-        q = ((ox + 4 * t + 254) % 256) // 2
-        q = (q + (mine - q + 128) % 8) % 128
-        z, h = (q // 8) % 8, q // 64
-        where[slot, 0:6] = summed[z, h, 0:6]
-        where[slot, 6] = jnp.where(level < 6, lines, summed[z, h, 6])
-
-    copies = []
-    j = 0
-    for device, dx, dh, dl in cross:
-        if dl == 0:
-            pick(device, sends, j)
-            copies.append(send(sends.at[j], ready.at[mine], sem2_s.at[j], sem2_r.at[j], device))
-            j += 1
-    pick(here, ready, mine)
-    store.wait()
-    for copy in copies:
-        copy.wait()
-
-    for k in range(8):
-        extra[6 * k : 6 * k + 6, :] = ready[k, 6, 0:6, :]
-
-    def place(j):
-        residue = (ox + 4 * tile + 254 + j) % 256
-        return (residue // 2) % 8, residue % 2
-
-    for j in range(9):
-        k, par = place(j)
-        for f in range(3):
-            old[j, pl.ds(8 * f, 8), :] = ready[k, 3 * par + f]
-
-    @pl.when(tile == 0)
-    def _():
-        old[1] = extra[0:24, :]
-
-    @pl.when(tile == 63)
-    def _():
-        old[6] = extra[24:48, :]
-
-    for j in range(1, 8):
-        k, par = place(j)
-        line = jnp.broadcast_to(ready[k, 6][6:7, :], (LEV, LANES))
-
-        def beyond(which):
-            def column(f):
-                at = 12 * level + 4 * f + 2 * par + which
-                return spread_out(jnp.sum(jnp.where(lane == at, line, 0.0), axis=1, keepdims=True))
-
-            return column
-
-        read = lambda i: lambda f, q: old[i, pl.ds(8 * f, 8), :]
-        for q, done in advance(coef, 1, read(j - 1), read(j), read(j + 1), beyond(0), beyond(1)):
-            for f in range(3):
-                new[j - 1, pl.ds(8 * f, 8), :] = done[f]
-
-    @pl.when(tile == 63)
-    def _():
-        old[6] = old[5]
-        new[5] = new[4]
-
-    for j in range(7):
-        part = jnp.concatenate([old[j + 1], (new[j] - old[j + 1]) * (1.0 / NSTEP)], axis=0)
-        for i in range(3):
-            rounded = part.astype(jnp.bfloat16)
-            flat[pl.ds(48 * j, 48), LANES * i : LANES * (i + 1)] = rounded
-            part = part - rounded.astype(F32)
-    wide[...] = jnp.dot(flat[...], mixer[...], preferred_element_type=F32).reshape(7, 2 * chan, width)
-
-    def pulls(u, carry):
-        for q in range(blocks):
-            columns = pl.ds(LANES * q, LANES)
-            for f in range(3):
-                at, to = pl.ds(8 * f, 8), pl.ds(chan + 8 * f, 8)
-                from_old, from_change = wide[u, at, columns], wide[u, to, columns]
-                over_old, over_change = wide[u + 1, at, columns] - from_old, wide[u + 1, to, columns] - from_change
-                for p in range(4):
-                    i = 4 * u + p
-                    p_row = pull[i, :, columns]
-                    now, change = (from_old, from_change) if p == 0 else (from_old + 0.25 * p * over_old, from_change + 0.25 * p * over_change)
-                    now, change = p_row * now, p_row * change
-                    base[i, at, columns] = now
-                    drift[i, at, columns] = change
-                    state_b[i, at, columns] = keep[i, :, columns] * state_b[i, at, columns] + (now + change)
-        return carry
-
-    state_b[0] = jnp.zeros((chan, width), F32)
-    state_b[tall - 1] = jnp.zeros((chan, width), F32)
-    lax.fori_loop(0, tall // 4, pulls, 0)
-
-    def step_pairs(src, dst, step, first):
-        def pair(m, carry):
-            for i in (first + 2 * m, first + 2 * m + 1):
-                for q, done in nest_row(src, i):
-                    columns = pl.ds(LANES * q, LANES)
-                    k_row = keep[i, :, columns]
-                    for f in range(3):
-                        at = pl.ds(8 * f, 8)
-                        dst[i, at, columns] = k_row * done[f] + (base[i, at, columns] + float(step) * drift[i, at, columns])
-            return carry
-
-        return pair
-
-    lax.fori_loop(0, (tall - 4) // 2, step_pairs(state_b, state_a, 2, 2), 0)
-    lax.fori_loop(0, (tall - 6) // 2, step_pairs(state_a, state_b, 3, 3), 0)
-    half = span // 2
-    parts = []
-    for part in range(2):
-        lax.fori_loop(0, half // 2, step_pairs(state_b, state_a, 4, NSTEP + half * part), 0)
-        parts.append(pltpu.make_async_copy(state_a.at[pl.ds(NSTEP + half * part, half)], nest_out.at[0, pl.ds(half * part, half)], sem_l.at[2 + part]))
-        parts[-1].start()
-    for copy in parts:
-        copy.wait()
+    finish = pltpu.make_async_copy(ready, slots_out, sem_l.at[7])
+    finish.start()
+    finish.wait()
 
 
 def fill_coefs(coef, diffusion, wind, conversion, mix):
@@ -518,6 +429,135 @@
         yield q, physics(coef, *moved)
 
 
+def nest_row(coef, src, i):
+    zero = jnp.zeros((LEV, LANES), F32)
+    read = lambda k: lambda f, q: src[k, pl.ds(8 * f, 8), pl.ds(LANES * q, LANES)]
+    yield from advance(coef, src.shape[2] // LANES, read(i - 1), read(i), read(i + 1), lambda f: zero, lambda f: zero)
+
+
+def nest_kernel(box, slots, moved, keep_in, pull_in, mixer_in, coef_in, parent_step, nest_out, parent_out, ready, state_b, keep, pull,
+                mixer, coef, state_a, passed, extra, old, new, flat, wide, base, drift, sem):
+    first = [pltpu.make_async_copy(slots, ready, sem.at[0]), pltpu.make_async_copy(coef_in, coef, sem.at[1])]
+    rest = [
+        pltpu.make_async_copy(moved, state_b, sem.at[2]),
+        pltpu.make_async_copy(keep_in, keep, sem.at[3]),
+        pltpu.make_async_copy(pull_in, pull, sem.at[4]),
+        pltpu.make_async_copy(mixer_in, mixer, sem.at[5]),
+    ]
+    take = pltpu.make_async_copy(parent_step, passed, sem.at[6])
+    give = pltpu.make_async_copy(passed, parent_out, sem.at[7])
+    for copy in first + rest[3:] + rest[:3] + [take]:
+        copy.start()
+    tile = tile_number()
+    ox = box[section(), 0]
+    tall, chan, width = state_a.shape
+    span = tall - 2 * NSTEP
+    blocks = width // LANES
+    lane = lane_ids()
+    level = level_ids()
+    for copy in first:
+        copy.wait()
+
+    for k in range(8):
+        extra[6 * k : 6 * k + 6, :] = ready[k, 6, 0:6, :]
+
+    def place(j):
+        residue = (ox + 4 * tile + 254 + j) % 256
+        return (residue // 2) % 8, residue % 2
+
+    for j in range(9):
+        k, par = place(j)
+        for f in range(3):
+            old[j, pl.ds(8 * f, 8), :] = ready[k, 3 * par + f]
+
+    @pl.when(tile == 0)
+    def _():
+        old[1] = extra[0:24, :]
+
+    @pl.when(tile == 63)
+    def _():
+        old[6] = extra[24:48, :]
+
+    for j in range(1, 8):
+        k, par = place(j)
+        line = jnp.broadcast_to(ready[k, 6][6:7, :], (LEV, LANES))
+
+        def beyond(which):
+            def column(f):
+                at = 12 * level + 4 * f + 2 * par + which
+                return spread_out(jnp.sum(jnp.where(lane == at, line, 0.0), axis=1, keepdims=True))
+
+            return column
+
+        read = lambda i: lambda f, q: old[i, pl.ds(8 * f, 8), :]
+        for q, done in advance(coef, 1, read(j - 1), read(j), read(j + 1), beyond(0), beyond(1)):
+            for f in range(3):
+                new[j - 1, pl.ds(8 * f, 8), :] = done[f]
+
+    @pl.when(tile == 63)
+    def _():
+        old[6] = old[5]
+        new[5] = new[4]
+
+    for j in range(7):
+        part = jnp.concatenate([old[j + 1], (new[j] - old[j + 1]) * (1.0 / NSTEP)], axis=0)
+        for i in range(3):
+            rounded = part.astype(jnp.bfloat16)
+            flat[pl.ds(48 * j, 48), LANES * i : LANES * (i + 1)] = rounded
+            part = part - rounded.astype(F32)
+    rest[3].wait()
+    wide[...] = jnp.dot(flat[...], mixer[...], preferred_element_type=F32).reshape(7, 2 * chan, width)
+
+    take.wait()
+    give.start()
+
+    def pulls(u, carry):
+        for q in range(blocks):
+            columns = pl.ds(LANES * q, LANES)
+            for f in range(3):
+                at, to = pl.ds(8 * f, 8), pl.ds(chan + 8 * f, 8)
+                from_old, from_change = wide[u, at, columns], wide[u, to, columns]
+                over_old, over_change = wide[u + 1, at, columns] - from_old, wide[u + 1, to, columns] - from_change
+                for p in range(4):
+                    i = 4 * u + p
+                    p_row = pull[i, :, columns]
+                    now, change = (from_old, from_change) if p == 0 else (from_old + 0.25 * p * over_old, from_change + 0.25 * p * over_change)
+                    now, change = p_row * now, p_row * change
+                    base[i, at, columns] = now
+                    drift[i, at, columns] = change
+                    state_b[i, at, columns] = keep[i, :, columns] * state_b[i, at, columns] + (now + change)
+        return carry
+
+    for copy in rest[:3]:
+        copy.wait()
+    lax.fori_loop(0, tall // 4, pulls, 0)
+
+    def step_pairs(src, dst, step, first):
+        def pair(m, carry):
+            for i in (first + 2 * m, first + 2 * m + 1):
+                for q, done in nest_row(coef, src, i):
+                    columns = pl.ds(LANES * q, LANES)
+                    k_row = keep[i, :, columns]
+                    for f in range(3):
+                        at = pl.ds(8 * f, 8)
+                        dst[i, at, columns] = k_row * done[f] + (base[i, at, columns] + float(step) * drift[i, at, columns])
+            return carry
+
+        return pair
+
+    lax.fori_loop(0, (tall - 4) // 2, step_pairs(state_b, state_a, 2, 2), 0)
+    lax.fori_loop(0, (tall - 6) // 2, step_pairs(state_a, state_b, 3, 3), 0)
+    half = span // 2
+    parts = []
+    for part in range(2):
+        lax.fori_loop(0, half // 2, step_pairs(state_b, state_a, 4, NSTEP + half * part), 0)
+        parts.append(pltpu.make_async_copy(state_a.at[pl.ds(NSTEP + half * part, half)], nest_out.at[0, pl.ds(half * part, half)], sem.at[8 + part]))
+        parts[-1].start()
+    for copy in parts:
+        copy.wait()
+    give.wait()
+
+
 def body(parent_old, nest_state, diffusion, wind_speed, conversion, vert_mix, nest_box):
     rows, chan, cols = parent_old.shape
     span, width = nest_state.shape[1], nest_state.shape[3]
@@ -528,24 +568,39 @@
     def room(*dims, kind=F32):
         return pltpu.VMEM(dims, kind)
 
-    return pl.pallas_call(
+    parent_step, slots, moved, keep, pull, mixer, coef = pl.pallas_call(
         step_kernel,
-        out_shape=(shape(parent_old.shape, F32), shape(nest_state.shape, F32)),
+        out_shape=(
+            shape(parent_old.shape, F32), shape((8, *SLOT), F32), shape((tall, chan, width), F32), shape((tall, LEV, width), F32),
+            shape((tall, LEV, width), F32), shape((3 * LANES, width), jnp.bfloat16), shape((3, 13, LEV, LANES), F32),
+        ),
         in_specs=[smem()] * 5 + [anywhere()] * 2,
-        out_specs=(anywhere(), anywhere()),
+        out_specs=(anywhere(),) * 7,
         scratch_shapes=[
             room(4, 8, *SLOT), room(2, chan, LANES), room(2, 8, *SLOT), room(2, 8, *SLOT), room(4, 2, 2, *SLOT), room(8, 2, *SLOT),
             room(8, *SLOT), room(7, *SLOT), room(2, chan, cols), room(2, chan, LANES),
             room(cols // LANES + 5, rows, chan, LANES), room(48, LANES), room(3, 13, LEV, LANES), room(rows, chan, cols),
             room(span, chan, width), room(NSTEP, chan, width), room(NSTEP, chan, width), room(tall, chan, width), room(tall, chan, width),
             room(tall, LEV, width), room(tall, LEV, width), room(3 * LANES, width, kind=jnp.bfloat16),
-            room(9, chan, LANES), room(7, chan, LANES), room(14 * chan, 3 * LANES, kind=jnp.bfloat16), room(7, 2 * chan, width),
-            room(tall, chan, width), room(tall, chan, width),
-            dma((7,)), dma((7,)), dma((15,)), dma((15,)), dma((7,)), dma((7,)), dma((7,)), dma((7,)), dma((cols // LANES,)), dma((4,)),
+            dma((7,)), dma((7,)), dma((15,)), dma((15,)), dma((7,)), dma((7,)), dma((7,)), dma((7,)), dma((cols // LANES,)), dma((8,)),
         ],
         compiler_params=pltpu.CompilerParams(collective_id=0, has_side_effects=True),
         name="step",
     )(nest_box, diffusion, wind_speed, conversion, vert_mix, nest_state, parent_old)
+    nest_new, parent_new = pl.pallas_call(
+        nest_kernel,
+        out_shape=(shape(nest_state.shape, F32), shape(parent_old.shape, F32)),
+        in_specs=[smem()] + [anywhere()] * 7,
+        out_specs=(anywhere(), anywhere()),
+        scratch_shapes=[
+            room(8, *SLOT), room(tall, chan, width), room(tall, LEV, width), room(tall, LEV, width),
+            room(3 * LANES, width, kind=jnp.bfloat16), room(3, 13, LEV, LANES), room(tall, chan, width), room(rows, chan, cols),
+            room(48, LANES), room(9, chan, LANES), room(7, chan, LANES), room(14 * chan, 3 * LANES, kind=jnp.bfloat16),
+            room(7, 2 * chan, width), room(tall, chan, width), room(tall, chan, width), dma((10,)),
+        ],
+        name="nest",
+    )(nest_box, slots, moved, keep, pull, mixer, coef, parent_step)
+    return parent_new, nest_new
 
 
 def solution(mesh):

time: 63.1 us -> 55.2 us (0.87)
  Pallas kernels: 58.6 us -> 54.4 us
  local copies, waits for them, and re-layouts: 3.68 us -> 0 us
    pallas_call x1, Pallas kernels: 58.6 us -> 45.3 us  [body(): pl.pallas_call(step_kernel, out_shape=(shape(parent_old.shape, F32), shap...]
    pallas_call x0 -> x1, Pallas kernels: none -> 9.14 us  [body(): pl.pallas_call(nest_kernel, out_shape=(shape(nest_state.shape, F32), shap...]
    unnamed x4 -> x0, local copies, waits for them, and re-layouts: 3.68 us -> none
where the time goes in v4:
time: 55.2 us; the launch traced here: 55.1 us
  Pallas kernels  54.4 us (99%)
  between operations  0.64 us (1%)
    pallas_call x1, Pallas kernels, body(): pl.pallas_call(step_kernel, out_shape=(shape(parent_old.shape, F32), shap...  45.3 us
    pallas_call x1, Pallas kernels, body(): pl.pallas_call(nest_kernel, out_shape=(shape(nest_state.shape, F32), shap...  9.14 us

profile of v4, /device:TPU:1, one launch (start us, length us, event | category | flops | bytes accessed | tf_op | source)
XLA Modules:
  0.0 55.1 jit_solution(3568743052432115454)
XLA Ops:
  0.6 45.3 %step.1 = (f32[16,24,1024]{2,1,0:T(8,128)}, f32[8,7,8,128]{3,2,1,0:T(8,128)}, f32[24,24,512]{2,1,0:T(8,128)}, f32[24,8,512]{2,1,0:T(8,128)}, f32[24,8,512]{2,1,0...) custom-call(s32[4,4]{1,0:T(4,128)} %box.3, f32[24]{0:T(128)} %diffusion.1, f32[2,24]{1,0:T(2,128)} %wind.1, ...), custom_call_target="tpu_custom_call" | custom-call | tf_op jit(solution)/shard_map/step/pallas_call | solution.py:571
  45.9 9.1 %nest.3 = (f32[1,16,24,512]{3,2,1,0:T(8,128)}, f32[16,24,1024]{2,1,0:T(8,128)}) custom-call(s32[4,4]{1,0:T(4,128)} %box.3, f32[8,7,8,128]{3,2,1,0:T(8,128)} %get-tuple-element.11.slots, f32[24,24,512]{2,1,0:T(8,128)} %get-tuple-element.12.moved, f32[24,8,512]{2,1,0:T(8,128)} %get-tuple-element.13.keep_in, f32[24,8,512]{2,1,0:T(8,128)} %get-tuple-element.14.pull_in, ...), custom_call_target="tpu_custom_call" | custom-call | tf_op jit(solution)/shard_map/nest/pallas_call | solution.py:590

commit v5 on v4

--- a/solution.py
+++ b/solution.py
@@ -136,7 +136,7 @@
     east, west = sec_at((sec + 1) % 4), sec_at((sec + 3) % 4)
     cross = [
         (dict(here, tx=(tx + dx) % 4, th=(th + dh) % 2, yl=(yl + dl) % 2), dx, dh, dl)
-        for dx, dh, dl in itertools.product((2, 1, 3, 0), (1, 0), (1, 0))
+        for dh, dx, dl in itertools.product((0, 1), (2, 1, 3, 0), (1, 0))
         if (dx, dh, dl) != (0, 0, 0)
     ]
     ring = [dict(here, tz=(tz + dz) % 8) for dz in (4, 3, 5, 2, 6, 1, 7)]
@@ -235,6 +235,24 @@
         copy.wait()
     lax.fori_loop(1, rows - 1, parent_rows, 0)
 
+    def gather(half, part):
+        for copy in part:
+            copy.wait()
+        total = gathered[0, 0, half]
+        for x, l in itertools.product(range(4), range(2)):
+            if (x, l) != (0, 0):
+                total = total + gathered[x, l, half]
+        summed[tz, half] = total
+
+    def around(half, which):
+        return [
+            send(summed.at[tz, half], summed.at[tz, half], semz_s.at[7 * which + j], semz_r.at[7 * which + j], device)
+            for j, device in enumerate(ring)
+        ]
+
+    gather(th, copies[:7])
+    rounds = around(th, 0)
+
     ox, ex, ey = box[sec, 0], box[sec, 2], box[sec, 3]
     row_id = span * tile - NSTEP + lax.broadcasted_iota(jnp.int32, (tall, width), 0)
     col_id = lax.broadcasted_iota(jnp.int32, (tall, width), 1)
@@ -258,6 +276,9 @@
     load_own.wait()
     lax.fori_loop(0, span, begin_own, 0)
 
+    gather(1 - th, copies[7:])
+    rounds += around(1 - th, 1)
+
     def first_row(i):
         for q, done in nest_row(coef, state_a, i):
             for f in range(3):
@@ -282,16 +303,6 @@
     for i in range(3):
         mixer[LANES * i : LANES * (i + 1), :] = mixed
 
-    for copy in copies:
-        copy.wait()
-    for h in range(2):
-        total = gathered[0, 0, h]
-        for x, l in itertools.product(range(4), range(2)):
-            if (x, l) != (0, 0):
-                total = total + gathered[x, l, h]
-        summed[tz, h] = total
-
-    copies = [send(summed.at[tz], summed.at[tz], semz_s.at[j], semz_r.at[j], device) for j, device in enumerate(ring)]
     out_moved, out_keep, out_pull = (
         pltpu.make_async_copy(src, dst, sem_l.at[i])
         for i, (src, dst) in enumerate(((state_b, moved_out), (keep, keep_out), (pull, pull_out)), 2)
@@ -302,7 +313,7 @@
     out_mixer.start()
     out_coef = pltpu.make_async_copy(coef, coef_out, sem_l.at[6])
     out_coef.start()
-    for copy in copies:
+    for copy in rounds:
         copy.wait()
 
     lines = summed[0, 0, 6]
@@ -320,7 +331,7 @@
 
     copies = []
     j = 0
-    for device, dx, dh, dl in cross:
+    for device, dx, dh, dl in cross[::-1]:
         if dl == 0:
             pick(device, sends, j)
             copies.append(send(sends.at[j], ready.at[mine], sem2_s.at[j], sem2_r.at[j], device))
@@ -361,49 +372,51 @@
             out = jnp.where(level == l, read(l), out)
         return out
 
+    spread, scale = [], []
     for f in range(3):
         d = column(lambda l: diffusion[8 * f + l])
         wx = column(lambda l: wind[0, 8 * f + l])
         wy = column(lambda l: wind[1, 8 * f + l])
-        coef[f, 0] = 1.0 - 4.0 * d - wx - wy
-        coef[f, 1] = d + wx
-        coef[f, 2] = d
-        coef[f, 3] = d + wy
+        coef[f, 0] = (1.0 - 4.0 * d - wx - wy) / d
+        coef[f, 1] = (d + wx) / d
+        coef[f, 2] = (d + wy) / d
         m = mix[f] * jnp.ones((LEV, LANES), F32)
         lower = jnp.where(level > 0, -m, 0.0)
         upper = jnp.where(level < LEV - 1, -m, 0.0)
         diag = 1.0 + m * jnp.where((level == 0) | (level == LEV - 1), 1.0, 2.0)
-        item = 7
+        steps = []
         for s in (1, 2, 4):
             alpha = -lower / pltpu.roll(diag, s, 0)
             gamma = -upper / pltpu.roll(diag, LEV - s, 0)
             new_diag = diag + alpha * pltpu.roll(upper, s, 0) + gamma * pltpu.roll(lower, LEV - s, 0)
             lower, upper = alpha * pltpu.roll(lower, s, 0), gamma * pltpu.roll(upper, LEV - s, 0)
             diag = new_diag
-            if s < 4:
-                coef[f, item] = alpha
-                coef[f, item + 1] = gamma
-                item += 2
-            else:
-                coef[f, item] = 1.0 / diag
-                coef[f, item + 1] = (alpha + gamma) / diag
+            steps.append((alpha, gamma))
+        for n, s in enumerate((1, 2)):
+            coef[f, 5 + 2 * n] = steps[n][0] * pltpu.roll(diag, s, 0) / diag
+            coef[f, 6 + 2 * n] = steps[n][1] * pltpu.roll(diag, LEV - s, 0) / diag
+        coef[f, 9] = (steps[2][0] + steps[2][1]) * pltpu.roll(diag, 4, 0) / diag
+        spread.append(d)
+        scale.append(1.0 / diag)
     c0 = column(lambda l: conversion[0, l])
     c1 = column(lambda l: conversion[1, l])
-    coef[0, 4] = c0
-    coef[0, 5] = 1.0 - c0
-    coef[1, 4] = c1
-    coef[1, 5] = 1.0 - c1
+    coef[0, 3] = c0 * spread[0]
+    coef[0, 4] = scale[0] * (1.0 - c0) * spread[0]
+    coef[1, 3] = spread[1]
+    coef[1, 4] = scale[1] * (1.0 - c1)
+    coef[2, 3] = scale[2] * spread[2]
+    coef[2, 4] = scale[2] * c1
 
 
 def solve(coef, f, r):
-    r = r + coef[f, 7] * pltpu.roll(r, 1, 0) + coef[f, 8] * pltpu.roll(r, 7, 0)
-    r = r + coef[f, 9] * pltpu.roll(r, 2, 0) + coef[f, 10] * pltpu.roll(r, 6, 0)
-    return coef[f, 11] * r + coef[f, 12] * pltpu.roll(r, 4, 0)
+    r = r + coef[f, 5] * pltpu.roll(r, 1, 0) + coef[f, 6] * pltpu.roll(r, 7, 0)
+    r = r + coef[f, 7] * pltpu.roll(r, 2, 0) + coef[f, 8] * pltpu.roll(r, 6, 0)
+    return r + coef[f, 9] * pltpu.roll(r, 4, 0)
 
 
 def physics(coef, vapour, cloud, rain):
-    wet = cloud + coef[0, 4] * vapour
-    fields = (coef[0, 5] * vapour, coef[1, 5] * wet, rain + coef[1, 4] * wet)
+    wet = coef[1, 3] * cloud + coef[0, 3] * vapour
+    fields = (coef[0, 4] * vapour, coef[1, 4] * wet, coef[2, 3] * rain + coef[2, 4] * wet)
     return [solve(coef, f, fields[f]) for f in range(3)]
 
 
@@ -425,7 +438,7 @@
                 read(f, q + 1)
             west = jnp.where(lane == 0, first(f) if q == 0 else right[f, q - 1], right[f, q])
             east = jnp.where(lane == LANES - 1, last(f) if q == count - 1 else left[f, q + 1], left[f, q])
-            moved.append(coef[f, 0] * tile[f, q] + coef[f, 1] * north(f, q) + coef[f, 2] * (south(f, q) + east) + coef[f, 3] * west)
+            moved.append((south(f, q) + east) + coef[f, 0] * tile[f, q] + coef[f, 1] * north(f, q) + coef[f, 2] * west)
         yield q, physics(coef, *moved)
 
 
@@ -436,7 +449,7 @@
 
 
 def nest_kernel(box, slots, moved, keep_in, pull_in, mixer_in, coef_in, parent_step, nest_out, parent_out, ready, state_b, keep, pull,
-                mixer, coef, state_a, passed, extra, old, new, flat, wide, base, drift, sem):
+                mixer, coef, state_a, passed, extra, old, new, flat, wide, base, base_b, drift, sem):
     first = [pltpu.make_async_copy(slots, ready, sem.at[0]), pltpu.make_async_copy(coef_in, coef, sem.at[1])]
     rest = [
         pltpu.make_async_copy(moved, state_b, sem.at[2]),
@@ -523,34 +536,39 @@
                     p_row = pull[i, :, columns]
                     now, change = (from_old, from_change) if p == 0 else (from_old + 0.25 * p * over_old, from_change + 0.25 * p * over_change)
                     now, change = p_row * now, p_row * change
-                    base[i, at, columns] = now
+                    now = now + change
+                    base[i, at, columns] = now + change
                     drift[i, at, columns] = change
-                    state_b[i, at, columns] = keep[i, :, columns] * state_b[i, at, columns] + (now + change)
+                    state_b[i, at, columns] = keep[i, :, columns] * state_b[i, at, columns] + now
         return carry
 
     for copy in rest[:3]:
         copy.wait()
     lax.fori_loop(0, tall // 4, pulls, 0)
 
-    def step_pairs(src, dst, step, first):
-        def pair(m, carry):
-            for i in (first + 2 * m, first + 2 * m + 1):
+    def step_rows(src, dst, first, group, here, there):
+        def several(m, carry):
+            for i in range(group):
+                i = first + group * m + i
                 for q, done in nest_row(coef, src, i):
                     columns = pl.ds(LANES * q, LANES)
                     k_row = keep[i, :, columns]
                     for f in range(3):
                         at = pl.ds(8 * f, 8)
-                        dst[i, at, columns] = k_row * done[f] + (base[i, at, columns] + float(step) * drift[i, at, columns])
+                        now = here[i, at, columns]
+                        dst[i, at, columns] = k_row * done[f] + now
+                        if there is not None:
+                            there[i, at, columns] = now + drift[i, at, columns]
             return carry
 
-        return pair
-
-    lax.fori_loop(0, (tall - 4) // 2, step_pairs(state_b, state_a, 2, 2), 0)
-    lax.fori_loop(0, (tall - 6) // 2, step_pairs(state_a, state_b, 3, 3), 0)
+        return several
+
+    lax.fori_loop(0, (tall - 4) // 4, step_rows(state_b, state_a, 2, 4, base, base_b), 0)
+    lax.fori_loop(0, (tall - 6) // 6, step_rows(state_a, state_b, 3, 6, base_b, base), 0)
     half = span // 2
     parts = []
     for part in range(2):
-        lax.fori_loop(0, half // 2, step_pairs(state_b, state_a, 4, NSTEP + half * part), 0)
+        lax.fori_loop(0, half // 4, step_rows(state_b, state_a, NSTEP + half * part, 4, base, None), 0)
         parts.append(pltpu.make_async_copy(state_a.at[pl.ds(NSTEP + half * part, half)], nest_out.at[0, pl.ds(half * part, half)], sem.at[8 + part]))
         parts[-1].start()
     for copy in parts:
@@ -572,17 +590,17 @@
         step_kernel,
         out_shape=(
             shape(parent_old.shape, F32), shape((8, *SLOT), F32), shape((tall, chan, width), F32), shape((tall, LEV, width), F32),
-            shape((tall, LEV, width), F32), shape((3 * LANES, width), jnp.bfloat16), shape((3, 13, LEV, LANES), F32),
+            shape((tall, LEV, width), F32), shape((3 * LANES, width), jnp.bfloat16), shape((3, 10, LEV, LANES), F32),
         ),
         in_specs=[smem()] * 5 + [anywhere()] * 2,
         out_specs=(anywhere(),) * 7,
         scratch_shapes=[
             room(4, 8, *SLOT), room(2, chan, LANES), room(2, 8, *SLOT), room(2, 8, *SLOT), room(4, 2, 2, *SLOT), room(8, 2, *SLOT),
             room(8, *SLOT), room(7, *SLOT), room(2, chan, cols), room(2, chan, LANES),
-            room(cols // LANES + 5, rows, chan, LANES), room(48, LANES), room(3, 13, LEV, LANES), room(rows, chan, cols),
+            room(cols // LANES + 5, rows, chan, LANES), room(48, LANES), room(3, 10, LEV, LANES), room(rows, chan, cols),
             room(span, chan, width), room(NSTEP, chan, width), room(NSTEP, chan, width), room(tall, chan, width), room(tall, chan, width),
             room(tall, LEV, width), room(tall, LEV, width), room(3 * LANES, width, kind=jnp.bfloat16),
-            dma((7,)), dma((7,)), dma((15,)), dma((15,)), dma((7,)), dma((7,)), dma((7,)), dma((7,)), dma((cols // LANES,)), dma((8,)),
+            dma((7,)), dma((7,)), dma((15,)), dma((15,)), dma((14,)), dma((14,)), dma((7,)), dma((7,)), dma((cols // LANES,)), dma((8,)),
         ],
         compiler_params=pltpu.CompilerParams(collective_id=0, has_side_effects=True),
         name="step",
@@ -594,9 +612,9 @@
         out_specs=(anywhere(), anywhere()),
         scratch_shapes=[
             room(8, *SLOT), room(tall, chan, width), room(tall, LEV, width), room(tall, LEV, width),
-            room(3 * LANES, width, kind=jnp.bfloat16), room(3, 13, LEV, LANES), room(tall, chan, width), room(rows, chan, cols),
+            room(3 * LANES, width, kind=jnp.bfloat16), room(3, 10, LEV, LANES), room(tall, chan, width), room(rows, chan, cols),
             room(48, LANES), room(9, chan, LANES), room(7, chan, LANES), room(14 * chan, 3 * LANES, kind=jnp.bfloat16),
-            room(7, 2 * chan, width), room(tall, chan, width), room(tall, chan, width), dma((10,)),
+            room(7, 2 * chan, width), room(tall, chan, width), room(tall, chan, width), room(tall, chan, width), dma((10,)),
         ],
         name="nest",
     )(nest_box, slots, moved, keep, pull, mixer, coef, parent_step)

time: 55.2 us -> 53.6 us (0.971); the launches traced: 55.1 us -> 52.6 us
  Pallas kernels: 54.4 us -> 51.9 us
    pallas_call x1, Pallas kernels: 45.3 us -> 43.9 us  [body(): pl.pallas_call(step_kernel, out_shape=(shape(parent_old.shape, F32), shap...]
    pallas_call x1, Pallas kernels: 9.14 us -> 8.03 us  [body(): pl.pallas_call(nest_kernel, out_shape=(shape(nest_state.shape, F32), shap...]
where the time goes in v5:
time: 53.6 us; the launch traced here: 52.6 us
  Pallas kernels  51.9 us (97%)
  between operations  0.64 us (1%)
    pallas_call x1, Pallas kernels, body(): pl.pallas_call(step_kernel, out_shape=(shape(parent_old.shape, F32), shap...  43.9 us
    pallas_call x1, Pallas kernels, body(): pl.pallas_call(nest_kernel, out_shape=(shape(nest_state.shape, F32), shap...  8.03 us

profile of v5, /device:TPU:1, one launch (start us, length us, event | category | flops | bytes accessed | tf_op | source)
XLA Modules:
  0.0 52.6 jit_solution(7474474775738020833)
XLA Ops:
  0.6 43.9 %step.1 = (f32[16,24,1024]{2,1,0:T(8,128)}, f32[8,7,8,128]{3,2,1,0:T(8,128)}, f32[24,24,512]{2,1,0:T(8,128)}, f32[24,8,512]{2,1,0:T(8,128)}, f32[24,8,512]{2,1,0...) custom-call(s32[4,4]{1,0:T(4,128)} %box.3, f32[24]{0:T(128)} %diffusion.1, f32[2,24]{1,0:T(2,128)} %wind.1, ...), custom_call_target="tpu_custom_call" | custom-call | tf_op jit(solution)/shard_map/step/pallas_call | solution.py:589
  44.5 8.0 %nest.3 = (f32[1,16,24,512]{3,2,1,0:T(8,128)}, f32[16,24,1024]{2,1,0:T(8,128)}) custom-call(s32[4,4]{1,0:T(4,128)} %box.3, f32[8,7,8,128]{3,2,1,0:T(8,128)} %get-tuple-element.11.slots, f32[24,24,512]{2,1,0:T(8,128)} %get-tuple-element.12.moved, f32[24,8,512]{2,1,0:T(8,128)} %get-tuple-element.13.keep_in, f32[24,8,512]{2,1,0:T(8,128)} %get-tuple-element.14.pull_in, ...), custom_call_target="tpu_custom_call" | custom-call | tf_op jit(solution)/shard_map/nest/pallas_call | solution.py:608

commit v6 on v5

--- a/solution.py
+++ b/solution.py
@@ -76,15 +76,12 @@
 
     back = (LANES - shift) % LANES
 
-    def turned(piece):
-        return pltpu.roll(piece, back, 1)
-
     def window(r, f):
-        near = turned(pad[block, r, pl.ds(8 * f, 8), :])
-        next_piece = pad[block + 1, r, pl.ds(8 * f, 8), :]
-        far = turned(next_piece)
-        return jnp.where(lane + shift < LANES, near, far), near, far
-
+        near = pad[block, r, pl.ds(8 * f, 8), :]
+        far = pad[block + 1, r, pl.ds(8 * f, 8), :]
+        return pltpu.roll(jnp.where(lane >= shift, near, far), back, 1), near, far
+
+    beyond = (shift == LANES) & (lane == 0)
     for k in range(rows // 2):
         packed = jnp.zeros((LEV, LANES), F32)
         for par in range(2):
@@ -94,9 +91,13 @@
             for f in range(3):
                 inner, near, far = window(r, f)
                 win[order, k, 3 * par + f] = inner * keep
-                far = jnp.where(shift < LANES, far, pad[block + 2, r, pl.ds(8 * f, 8), :])
-                pair = jnp.where(lane % 2 == 0, spread_out(near[:, LANES - 1 : LANES]), spread_out(far[:, 0:1]))
-                packed = jnp.where(lane // 2 == 6 * level + 2 * f + par, pair * keep, packed)
+                sides = jnp.where(lane < shift, near, far)
+                sides = jnp.where(beyond, pad[block + 2, r, pl.ds(8 * f, 8), :], sides)
+                pair = 2 * f + par
+                sides = pltpu.roll(sides, (2 * pair + 1 + LANES - shift) % LANES, 1)
+                packed = jnp.where(lane // 2 == pair, sides * keep, packed)
+        for bit in (1, 2, 4):
+            packed = jnp.where((level // bit) % 2 == 1, pltpu.roll(packed, 12 * bit, 1), packed)
         line = jnp.sum(packed, axis=0, keepdims=True)
         win[order, k, 6] = jnp.where(level == 6, jnp.broadcast_to(line, (LEV, LANES)), 0.0)
 
@@ -233,7 +234,7 @@
 
     for copy in columns:
         copy.wait()
-    lax.fori_loop(1, rows - 1, parent_rows, 0)
+    lax.fori_loop(1, rows // 2, parent_rows, 0)
 
     def gather(half, part):
         for copy in part:
@@ -292,6 +293,7 @@
 
         return pair
 
+    lax.fori_loop(rows // 2, rows - 1, parent_rows, 0)
     lax.fori_loop(0, span // 2 - 1, first_rows(NSTEP + 1), 0)
 
     cells = lax.broadcasted_iota(jnp.int32, (LANES, width), 0)

time: 53.6 us -> 48.9 us (0.912)
  Pallas kernels: 51.9 us -> 47.5 us
    pallas_call x1, Pallas kernels: 43.9 us -> 39.4 us  [body(): pl.pallas_call(step_kernel, out_shape=(shape(parent_old.shape, F32), shap...]
where the time goes in v6:
time: 48.9 us; the launch traced here: 48.1 us
  Pallas kernels  47.5 us (97%)
  between operations  0.64 us (1%)
    pallas_call x1, Pallas kernels, body(): pl.pallas_call(step_kernel, out_shape=(shape(parent_old.shape, F32), shap...  39.4 us
    pallas_call x1, Pallas kernels, body(): pl.pallas_call(nest_kernel, out_shape=(shape(nest_state.shape, F32), shap...  8.03 us

profile of v6, /device:TPU:1, one launch (start us, length us, event | category | flops | bytes accessed | tf_op | source)
XLA Modules:
  0.0 48.1 jit_solution(13397801109016411288)
XLA Ops:
  0.6 39.4 %step.1 = (f32[16,24,1024]{2,1,0:T(8,128)}, f32[8,7,8,128]{3,2,1,0:T(8,128)}, f32[24,24,512]{2,1,0:T(8,128)}, f32[24,8,512]{2,1,0:T(8,128)}, f32[24,8,512]{2,1,0...) custom-call(s32[4,4]{1,0:T(4,128)} %box.3, f32[24]{0:T(128)} %diffusion.1, f32[2,24]{1,0:T(2,128)} %wind.1, ...), custom_call_target="tpu_custom_call" | custom-call | tf_op jit(solution)/shard_map/step/pallas_call | solution.py:591
  40.1 8.0 %nest.3 = (f32[1,16,24,512]{3,2,1,0:T(8,128)}, f32[16,24,1024]{2,1,0:T(8,128)}) custom-call(s32[4,4]{1,0:T(4,128)} %box.3, f32[8,7,8,128]{3,2,1,0:T(8,128)} %get-tuple-element.11.slots, f32[24,24,512]{2,1,0:T(8,128)} %get-tuple-element.12.moved, f32[24,8,512]{2,1,0:T(8,128)} %get-tuple-element.13.keep_in, f32[24,8,512]{2,1,0:T(8,128)} %get-tuple-element.14.pull_in, ...), custom_call_target="tpu_custom_call" | custom-call | tf_op jit(solution)/shard_map/nest/pallas_call | solution.py:610

commit v7 on v6

--- a/solution.py
+++ b/solution.py
@@ -82,6 +82,7 @@
         return pltpu.roll(jnp.where(lane >= shift, near, far), back, 1), near, far
 
     beyond = (shift == LANES) & (lane == 0)
+    from_left = (lane - shift + 1 + LANES) % LANES
     for k in range(rows // 2):
         packed = jnp.zeros((LEV, LANES), F32)
         for par in range(2):
@@ -94,8 +95,9 @@
                 sides = jnp.where(lane < shift, near, far)
                 sides = jnp.where(beyond, pad[block + 2, r, pl.ds(8 * f, 8), :], sides)
                 pair = 2 * f + par
-                sides = pltpu.roll(sides, (2 * pair + 1 + LANES - shift) % LANES, 1)
-                packed = jnp.where(lane // 2 == pair, sides * keep, packed)
+                sides = sides * keep
+                packed = jnp.where(from_left // 2 == pair, pltpu.roll(sides, 2 * pair, 1) if pair else sides, packed)
+        packed = pltpu.roll(packed, (1 + LANES - shift) % LANES, 1)
         for bit in (1, 2, 4):
             packed = jnp.where((level // bit) % 2 == 1, pltpu.roll(packed, 12 * bit, 1), packed)
         line = jnp.sum(packed, axis=0, keepdims=True)
@@ -112,7 +114,7 @@
 
 def step_kernel(box, diffusion, wind, conversion, mix, nest, parent, parent_out, slots_out, moved_out, keep_out, pull_out, mixer_out,
                 coef_out, win, edge, near, comb, gathered, summed,
-                ready, sends, rowhalo, colhalo, pad, extra, coef, result, own, low, high, state_a, state_b, keep, pull, mixer,
+                sends, rowhalo, colhalo, pad, extra, coef, result, own, low, high, state_a, state_b, keep, pull, mixer,
                 sem_s, sem_r, sem1_s, sem1_r, semz_s, semz_r, sem2_s, sem2_r, sem_p, sem_l):
     yl, co, tx, th, tz = (lax.axis_index(a) for a in ("yl", "co", "tx", "th", "tz"))
     mine = tx * 2 + th
@@ -190,26 +192,26 @@
     for copy in onward + backward:
         copy.start()
     lax.fori_loop(co * 2, co * 2 + 2, pack, 0)
+    first.wait()
+
+    def combine(k, carry):
+        for l in range(2):
+            comb[l, k] = win[co * 2 + l, k] + near[l, k]
+        return carry
+
+    lax.fori_loop(0, 8, combine, 0)
+
+    copies = []
+    for j, (device, dx, dh, dl) in enumerate(cross):
+        to = device["tx"] * 2 + device["th"]
+        copies.append(send(comb.at[device["yl"], to], gathered.at[tx, yl, th], sem1_s.at[j], sem1_r.at[j], device))
+    gathered[tx, yl, th] = comb[yl, mine]
     pack_edges(pad, edge, rows, count)
     columns = [
         send(edge.at[1], colhalo.at[0], sem_s.at[1], sem_r.at[1], east),
         send(edge.at[0], colhalo.at[1], sem_s.at[2], sem_r.at[2], west),
     ]
     fill_coefs(coef, diffusion, wind, conversion, mix)
-    first.wait()
-
-    def combine(k, carry):
-        for l in range(2):
-            comb[l, k] = win[co * 2 + l, k] + near[l, k]
-        return carry
-
-    lax.fori_loop(0, 8, combine, 0)
-
-    copies = []
-    for j, (device, dx, dh, dl) in enumerate(cross):
-        to = device["tx"] * 2 + device["th"]
-        copies.append(send(comb.at[device["yl"], to], gathered.at[tx, yl, th], sem1_s.at[j], sem1_r.at[j], device))
-    gathered[tx, yl, th] = comb[yl, mine]
 
     have = [jnp.where(c, 1.0, 0.0).astype(F32) for c in (tile > 0, tile < 63, sec > 0, sec < 3)]
 
@@ -231,28 +233,6 @@
     def parent_rows(i, carry):
         parent_row(i, inner(i - 1), inner(i + 1))
         return carry
-
-    for copy in columns:
-        copy.wait()
-    lax.fori_loop(1, rows // 2, parent_rows, 0)
-
-    def gather(half, part):
-        for copy in part:
-            copy.wait()
-        total = gathered[0, 0, half]
-        for x, l in itertools.product(range(4), range(2)):
-            if (x, l) != (0, 0):
-                total = total + gathered[x, l, half]
-        summed[tz, half] = total
-
-    def around(half, which):
-        return [
-            send(summed.at[tz, half], summed.at[tz, half], semz_s.at[7 * which + j], semz_r.at[7 * which + j], device)
-            for j, device in enumerate(ring)
-        ]
-
-    gather(th, copies[:7])
-    rounds = around(th, 0)
 
     ox, ex, ey = box[sec, 0], box[sec, 2], box[sec, 3]
     row_id = span * tile - NSTEP + lax.broadcasted_iota(jnp.int32, (tall, width), 0)
@@ -277,6 +257,29 @@
     load_own.wait()
     lax.fori_loop(0, span, begin_own, 0)
 
+    for copy in columns:
+        copy.wait()
+    lax.fori_loop(1, 5, parent_rows, 0)
+
+    def gather(half, part):
+        for copy in part:
+            copy.wait()
+        total = gathered[0, 0, half]
+        for x, l in itertools.product(range(4), range(2)):
+            if (x, l) != (0, 0):
+                total = total + gathered[x, l, half]
+        summed[tz, half] = total
+
+    def around(half, which):
+        return [
+            send(summed.at[tz, half], summed.at[tz, half], semz_s.at[7 * which + j], semz_r.at[7 * which + j], device)
+            for j, device in enumerate(ring)
+        ]
+
+    gather(th, copies[:7])
+    rounds = around(th, 0)
+
+    lax.fori_loop(5, rows // 2, parent_rows, 0)
     gather(1 - th, copies[7:])
     rounds += around(1 - th, 1)
 
@@ -336,9 +339,11 @@
     for device, dx, dh, dl in cross[::-1]:
         if dl == 0:
             pick(device, sends, j)
-            copies.append(send(sends.at[j], ready.at[mine], sem2_s.at[j], sem2_r.at[j], device))
+            copies.append(send(sends.at[j], slots_out.at[mine], sem2_s.at[j], sem2_r.at[j], device))
             j += 1
-    pick(here, ready, mine)
+    pick(here, sends, 7)
+    finish = pltpu.make_async_copy(sends.at[7], slots_out.at[mine], sem_l.at[7])
+    finish.start()
 
     onward[0].wait()
     backward[0].wait()
@@ -360,8 +365,6 @@
         copy.wait()
     for copy in copies:
         copy.wait()
-    finish = pltpu.make_async_copy(ready, slots_out, sem_l.at[7])
-    finish.start()
     finish.wait()
 
 
@@ -565,12 +568,12 @@
 
         return several
 
-    lax.fori_loop(0, (tall - 4) // 4, step_rows(state_b, state_a, 2, 4, base, base_b), 0)
+    lax.fori_loop(0, (tall - 4) // 10, step_rows(state_b, state_a, 2, 10, base, base_b), 0)
     lax.fori_loop(0, (tall - 6) // 6, step_rows(state_a, state_b, 3, 6, base_b, base), 0)
     half = span // 2
     parts = []
     for part in range(2):
-        lax.fori_loop(0, half // 4, step_rows(state_b, state_a, NSTEP + half * part, 4, base, None), 0)
+        lax.fori_loop(0, half // 8, step_rows(state_b, state_a, NSTEP + half * part, 8, base, None), 0)
         parts.append(pltpu.make_async_copy(state_a.at[pl.ds(NSTEP + half * part, half)], nest_out.at[0, pl.ds(half * part, half)], sem.at[8 + part]))
         parts[-1].start()
     for copy in parts:
@@ -598,7 +601,7 @@
         out_specs=(anywhere(),) * 7,
         scratch_shapes=[
             room(4, 8, *SLOT), room(2, chan, LANES), room(2, 8, *SLOT), room(2, 8, *SLOT), room(4, 2, 2, *SLOT), room(8, 2, *SLOT),
-            room(8, *SLOT), room(7, *SLOT), room(2, chan, cols), room(2, chan, LANES),
+            room(8, *SLOT), room(2, chan, cols), room(2, chan, LANES),
             room(cols // LANES + 5, rows, chan, LANES), room(48, LANES), room(3, 10, LEV, LANES), room(rows, chan, cols),
             room(span, chan, width), room(NSTEP, chan, width), room(NSTEP, chan, width), room(tall, chan, width), room(tall, chan, width),
             room(tall, LEV, width), room(tall, LEV, width), room(3 * LANES, width, kind=jnp.bfloat16),

time: 48.9 us -> 49.7 us (1.016)
  Pallas kernels: 47.5 us -> 48.3 us
    pallas_call x1, Pallas kernels: 39.4 us -> 40.8 us  [body(): pl.pallas_call(step_kernel, out_shape=(shape(parent_old.shape, F32), shap...]
where the time goes in v7:
time: 49.7 us; the launch traced here: 49 us
  Pallas kernels  48.3 us (97%)
  between operations  0.64 us (1%)
    pallas_call x1, Pallas kernels, body(): pl.pallas_call(step_kernel, out_shape=(shape(parent_old.shape, F32), shap...  40.8 us
    pallas_call x1, Pallas kernels, body(): pl.pallas_call(nest_kernel, out_shape=(shape(nest_state.shape, F32), shap...  7.57 us

profile of v7, /device:TPU:1, one launch (start us, length us, event | category | flops | bytes accessed | tf_op | source)
XLA Modules:
  0.0 49.0 jit_solution(9681838252609002432)
XLA Ops:
  0.6 40.8 %step.1 = (f32[16,24,1024]{2,1,0:T(8,128)}, f32[8,7,8,128]{3,2,1,0:T(8,128)}, f32[24,24,512]{2,1,0:T(8,128)}, f32[24,8,512]{2,1,0:T(8,128)}, f32[24,8,512]{2,1,0...) custom-call(s32[4,4]{1,0:T(4,128)} %box.3, f32[24]{0:T(128)} %diffusion.1, f32[2,24]{1,0:T(2,128)} %wind.1, ...), custom_call_target="tpu_custom_call" | custom-call | tf_op jit(solution)/shard_map/step/pallas_call | solution.py:594
  41.4 7.6 %nest.3 = (f32[1,16,24,512]{3,2,1,0:T(8,128)}, f32[16,24,1024]{2,1,0:T(8,128)}) custom-call(s32[4,4]{1,0:T(4,128)} %box.3, f32[8,7,8,128]{3,2,1,0:T(8,128)} %get-tuple-element.11.slots, f32[24,24,512]{2,1,0:T(8,128)} %get-tuple-element.12.moved, f32[24,8,512]{2,1,0:T(8,128)} %get-tuple-element.13.keep_in, f32[24,8,512]{2,1,0:T(8,128)} %get-tuple-element.14.pull_in, ...), custom_call_target="tpu_custom_call" | custom-call | tf_op jit(solution)/shard_map/nest/pallas_call | solution.py:613

commit v8 on v6

--- a/solution.py
+++ b/solution.py
@@ -82,6 +82,7 @@
         return pltpu.roll(jnp.where(lane >= shift, near, far), back, 1), near, far
 
     beyond = (shift == LANES) & (lane == 0)
+    from_left = (lane - shift + 1 + LANES) % LANES
     for k in range(rows // 2):
         packed = jnp.zeros((LEV, LANES), F32)
         for par in range(2):
@@ -94,8 +95,9 @@
                 sides = jnp.where(lane < shift, near, far)
                 sides = jnp.where(beyond, pad[block + 2, r, pl.ds(8 * f, 8), :], sides)
                 pair = 2 * f + par
-                sides = pltpu.roll(sides, (2 * pair + 1 + LANES - shift) % LANES, 1)
-                packed = jnp.where(lane // 2 == pair, sides * keep, packed)
+                sides = sides * keep
+                packed = jnp.where(from_left // 2 == pair, pltpu.roll(sides, 2 * pair, 1) if pair else sides, packed)
+        packed = pltpu.roll(packed, (1 + LANES - shift) % LANES, 1)
         for bit in (1, 2, 4):
             packed = jnp.where((level // bit) % 2 == 1, pltpu.roll(packed, 12 * bit, 1), packed)
         line = jnp.sum(packed, axis=0, keepdims=True)
@@ -565,12 +567,12 @@
 
         return several
 
-    lax.fori_loop(0, (tall - 4) // 4, step_rows(state_b, state_a, 2, 4, base, base_b), 0)
+    lax.fori_loop(0, (tall - 4) // 10, step_rows(state_b, state_a, 2, 10, base, base_b), 0)
     lax.fori_loop(0, (tall - 6) // 6, step_rows(state_a, state_b, 3, 6, base_b, base), 0)
     half = span // 2
     parts = []
     for part in range(2):
-        lax.fori_loop(0, half // 4, step_rows(state_b, state_a, NSTEP + half * part, 4, base, None), 0)
+        lax.fori_loop(0, half // 8, step_rows(state_b, state_a, NSTEP + half * part, 8, base, None), 0)
         parts.append(pltpu.make_async_copy(state_a.at[pl.ds(NSTEP + half * part, half)], nest_out.at[0, pl.ds(half * part, half)], sem.at[8 + part]))
         parts[-1].start()
     for copy in parts:

time: 48.9 us -> 49 us (level)
    pallas_call x1, Pallas kernels: 39.4 us -> 40.1 us  [body(): pl.pallas_call(step_kernel, out_shape=(shape(parent_old.shape, F32), shap...]
where the time goes in v8:
time: 49 us; the launch traced here: 48.3 us
  Pallas kernels  47.7 us (97%)
  between operations  0.64 us (1%)
    pallas_call x1, Pallas kernels, body(): pl.pallas_call(step_kernel, out_shape=(shape(parent_old.shape, F32), shap...  40.1 us
    pallas_call x1, Pallas kernels, body(): pl.pallas_call(nest_kernel, out_shape=(shape(nest_state.shape, F32), shap...  7.57 us

profile of v8, /device:TPU:1, one launch (start us, length us, event | category | flops | bytes accessed | tf_op | source)
XLA Modules:
  0.0 48.3 jit_solution(81692628176372197)
XLA Ops:
  0.6 40.1 %step.1 = (f32[16,24,1024]{2,1,0:T(8,128)}, f32[8,7,8,128]{3,2,1,0:T(8,128)}, f32[24,24,512]{2,1,0:T(8,128)}, f32[24,8,512]{2,1,0:T(8,128)}, f32[24,8,512]{2,1,0...) custom-call(s32[4,4]{1,0:T(4,128)} %box.3, f32[24]{0:T(128)} %diffusion.1, f32[2,24]{1,0:T(2,128)} %wind.1, ...), custom_call_target="tpu_custom_call" | custom-call | tf_op jit(solution)/shard_map/step/pallas_call | solution.py:593
  40.8 7.6 %nest.3 = (f32[1,16,24,512]{3,2,1,0:T(8,128)}, f32[16,24,1024]{2,1,0:T(8,128)}) custom-call(s32[4,4]{1,0:T(4,128)} %box.3, f32[8,7,8,128]{3,2,1,0:T(8,128)} %get-tuple-element.11.slots, f32[24,24,512]{2,1,0:T(8,128)} %get-tuple-element.12.moved, f32[24,8,512]{2,1,0:T(8,128)} %get-tuple-element.13.keep_in, f32[24,8,512]{2,1,0:T(8,128)} %get-tuple-element.14.pull_in, ...), custom_call_target="tpu_custom_call" | custom-call | tf_op jit(solution)/shard_map/nest/pallas_call | solution.py:612
